TPU v7x, 256 devices: a whole 4x4x8 slice. The times are simulated.
256 devices in a mesh: fsdp: 8 (over x_hi, y), ctx: 32 (over z, x_lo, core).
Axes of the slice: x: 4 (x_hi: 2, x_lo: 2; x = x_hi * 2 + x_lo), y: 4, z: 8, core: 2. Of those that a mesh axis runs over, the one named last changes fastest.
Arguments:
- tokens: bfloat16 [8, 4096, 1024], P('fsdp', 'ctx'), may hold values from -16 to 16
- cotangent: bfloat16 [8, 4096, 1024], P('fsdp', 'ctx'), may hold values from -6 to 6
- w_query: bfloat16 [1024, 512], P('fsdp')
- w_key: bfloat16 [1024, 512], P('fsdp')
- w_value: bfloat16 [1024, 512], P('fsdp'), may hold values from -0.1875 to 0.1875
- w_out: bfloat16 [512, 1024], P('fsdp'), may hold values from -0.25 to 0.25
- block_mask: int32 [32, 32], replicated, may hold values from 0 to 1, as said below
- span_order: int32 [64], replicated, may hold values from 0 to 63, each once
Outputs:
- mixed_out: bfloat16 [8, 4096, 1024], P('fsdp', 'ctx')
- token_grad: bfloat16 [8, 4096, 1024], P('fsdp', 'ctx')
- grad_query: float32 [1024, 512], P(('fsdp', 'ctx'))
- grad_key: float32 [1024, 512], P(('fsdp', 'ctx'))
- grad_value: float32 [1024, 512], P(('fsdp', 'ctx'))
- grad_out: float32 [512, 1024], P(('fsdp', 'ctx'))
Inputs may be any that keep to these rules, and one draw needn't show every extreme that they name: `block_mask`: every diagonal entry is 1.
All inputs are finite; a program needn't handle non-finite values.
Results may differ from a plain program's by a relative error of at most 0.013.
The roundings to bfloat16 on the way count: a program that leaves them out, or rounds other values in their place, can miss the bound.
Values may be sent and summed in bfloat16 or wider, within the bound.
No kernel may reach another device: no remote copies, remote signals or barrier semaphores. Data moves between devices by JAX's collectives and lax.ppermute only.
A program may use at most 128 MiB of HBM per device.

v0:
```python
import functools
import math

import jax
import jax.numpy as jnp
from jax import lax
from jax.experimental import pallas as pl
from jax.experimental.pallas import tpu as pltpu
from jax.sharding import Mesh
from jax.sharding import PartitionSpec as P

HEADS = 4
HD = 128
SPAN = 64
NF = 8
NZ = 8
ROWS = 512
NEG = -1e30
SCALE = 1.0 / math.sqrt(HD)
C2 = SCALE * math.log2(math.e)
FLOPS = 8
VMEM_LIMIT = 16 << 20
BF = jnp.bfloat16
F32 = jnp.float32


def dot(a, b):
    return jnp.dot(a, b, preferred_element_type=F32)


def dot_nt(a, b):
    return lax.dot_general(a, b, (((1,), (1,)), ((), ())), preferred_element_type=F32)


def dot_tn(a, b):
    return lax.dot_general(a, b, (((0,), (0,)), ((), ())), preferred_element_type=F32)


def with_bias(s, bias_ref, firsts):
    parts = []
    for t in range(ROWS // SPAN):
        row = jnp.concatenate([bias_ref[first + t] for first in firsts], axis=1)
        parts.append(s[t * SPAN : (t + 1) * SPAN, :] + row)
    return jnp.concatenate(parts, axis=0)


def tiles(s):
    return [s[:, t * HD : (t + 1) * HD] for t in range(s.shape[1] // HD)]


def wide(row, count):
    return jnp.concatenate([row] * (count * (ROWS // HD)), axis=1)


class Staged:
    def __init__(self, pieces, buf, sems, at_once):
        self.buf, self.sems = buf, sems
        self.turns, size = buf.shape[0], at_once * ROWS
        self.parts = [[] for _ in range(self.turns)]
        first = 0
        for n, piece in enumerate(pieces):
            turn, row = divmod(first, size)
            self.parts[turn].append((n, row, piece.shape[0]))
            pltpu.make_async_copy(
                piece, buf.at[turn, pl.ds(row, piece.shape[0])], sems.at[n]
            ).start()
            first += piece.shape[0]

    def turn(self, n):
        def wait(parts, number):
            for i, (_, row, rows) in enumerate(parts):
                block = self.buf.at[n, pl.ds(row, rows)]
                pltpu.make_async_copy(block, block, self.sems.at[number + i]).wait()

        usual = len(self.parts[0])
        if len(self.parts[-1]) == usual:
            wait(self.parts[0], n * usual)
        else:

            @pl.when(n < self.turns - 1)
            def _():
                wait(self.parts[0], n * usual)

            @pl.when(n == self.turns - 1)
            def _():
                wait(self.parts[-1], (self.turns - 1) * usual)

        return self.buf.at[n]


def forward_kernel(pieces, at_once, first, last, number_ref, *refs):
    q_ref, refs = refs[0], refs[1:]
    chunks, refs = refs[:pieces], refs[pieces:]
    bias_ref, refs = refs[0], refs[1:]
    if not first:
        state_in, refs = refs[0], refs[1:]
    if last:
        g_ref, o_ref, stat_ref, state, buf, sems = refs
    else:
        state, buf, sems = refs
    blocks = Staged(chunks, buf, sems, at_once)
    if first:
        state[0] = jnp.full_like(state[0], NEG)
        state[1] = jnp.zeros_like(state[1])
        state[2] = jnp.zeros_like(state[2])
    else:
        state[...] = state_in[...]

    @pl.loop(0, blocks.turns)
    def _(n):
        kv = blocks.turn(n)
        s = dot_nt(q_ref[...], kv[:, :HD]) * C2
        s = with_bias(s, bias_ref, [number_ref[n * at_once + i] * 8 for i in range(at_once)])
        old = state[0]
        top = functools.reduce(jnp.maximum, tiles(s))
        new = jnp.maximum(old, jnp.max(top, axis=1, keepdims=True))
        fade = jnp.exp2(old - new)
        e = jnp.exp2(s - wide(new, at_once))
        state[0] = new
        state[1] = state[1] * fade + sum(tiles(e))
        state[2] = state[2] * fade + dot(e.astype(BF), kv[:, HD:])

    if last:
        total = jnp.sum(state[1], axis=1, keepdims=True)
        combined = state[2] * (1.0 / total)
        o_ref[...] = combined.astype(BF)
        lse = state[0] + jnp.log2(total)
        delta = jnp.sum(combined * g_ref[...].astype(F32), axis=1, keepdims=True)
        delta = jnp.broadcast_to(delta, (ROWS, HD))
        stat_ref[0:1, :] = lse.T[0:1, :]
        stat_ref[1:2, :] = delta.T[0:1, :]


def backward_kernel(pieces, first, last, q_ref, g_ref, stat_ref, number_ref, *refs):
    chunks, refs = refs[:pieces], refs[pieces:]
    bias_ref, refs = refs[0], refs[1:]
    if not first:
        acc_in, refs = refs[0], refs[1:]
    part_ref, refs = refs[0], refs[1:]
    if last:
        dq_ref, acc, buf, sems = refs
    else:
        acc, buf, sems = refs
    blocks = Staged(chunks, buf, sems, 1)
    if first:
        acc[...] = jnp.zeros_like(acc)
    else:
        acc[...] = acc_in[...]

    @pl.loop(0, blocks.turns)
    def _(n):
        kv = blocks.turn(n)
        q = q_ref[...]
        g = g_ref[...]
        k = kv[:, :HD]
        s = dot_nt(k, q) * C2
        p = jnp.exp2(with_bias(s, bias_ref, [number_ref[n] * 8]) - stat_ref[0:1, :])
        dp = dot_nt(kv[:, HD:], g)
        ds = (p * (dp - stat_ref[1:2, :])).astype(BF)
        part_ref[n, :, :HD] = (dot(ds, q) * SCALE).astype(BF)
        part_ref[n, :, HD:] = dot(p.astype(BF), g).astype(BF)
        acc[...] += dot(k.T, ds)

    if last:
        dq_ref[...] = (acc[...] * SCALE).T.astype(BF)


def bring(blocks, buf, sems):
    size = blocks[0].shape[0]
    copies = [
        pltpu.make_async_copy(block, buf.at[pl.ds(d * size, size)], sems.at[d])
        for d, block in enumerate(blocks)
    ]
    for copy in copies:
        copy.start()
    return [copy.wait for copy in copies]


def tokens_kernel(*refs):
    blocks, (w_ref, kv_ref, q_ref, x_ref) = refs[:HEADS], refs[HEADS:]
    for d, block in enumerate(blocks):
        rows = pl.ds(d * block.shape[0], block.shape[0])
        x_ref[rows, :] = block[...]
        kvq = dot(block[...], w_ref[...]).astype(BF)
        kv_ref[rows, :] = kvq[:, : 2 * HD]
        q_ref[rows, :] = kvq[:, 2 * HD :]


def cotangent_kernel(f_ref, a_ref, b_ref, *refs):
    blocks, (g_ref, dy_ref, out_ref) = refs[:HEADS], refs[HEADS:]
    size = a_ref.shape[0]
    turned = f_ref[0] // (NF // 2) * size
    out_ref[pl.ds(pl.multiple_of(turned, size), size), :] = a_ref[...]
    out_ref[pl.ds(pl.multiple_of(size - turned, size), size), :] = b_ref[...]
    for d, block in enumerate(blocks):
        rows = pl.ds(d * block.shape[0], block.shape[0])
        dy_ref[rows, :] = block[...]
        g_ref[rows, :] = dot_nt(block[...], out_ref[...]).astype(BF)


def out_kernel(h_ref, *refs):
    blocks, (dy_ref, o_ref, att, dy, sems, sem) = refs[:HEADS], refs[HEADS:]
    h = h_ref[0]
    part = dy_ref.at[:, pl.ds(pl.multiple_of(h * 256, 256), 256)]
    copy = pltpu.make_async_copy(part, dy, sem)
    copy.start()
    waits = bring(blocks, att, sems)
    copy.wait()
    size = ROWS // HEADS
    for d, wait in enumerate(waits):
        wait()
        rows = jnp.concatenate(
            [att[d * ROWS + (i ^ d) * size : d * ROWS + (i ^ d) * size + size, :] for i in range(HEADS)],
            axis=0,
        )
        grad = dot_tn(rows, dy[...]).astype(BF)
        for e in range(2):
            for c in range(2):
                o_ref[2 * (h ^ d) + e, c * 64 : (c + 1) * 64, :] = grad[
                    e * 64 : (e + 1) * 64, c * HD : (c + 1) * HD
                ]


def heads_kernel(transposed, a_ref, w_ref, own_ref, send_ref):
    terms = (dot_nt if transposed else dot)(a_ref[...], w_ref[...])
    size = ROWS // HEADS
    for i in range(2):
        own_ref[i] = terms[2 * i * size : (2 * i + 1) * size]
        send_ref[i] = terms[(2 * i + 1) * size : (2 * i + 2) * size].astype(BF)


def chip_kernel(own_ref, got_ref, keep_ref, send_ref):
    keep_ref[...] = own_ref[0] + got_ref[0].astype(F32)
    send_ref[...] = (own_ref[1] + got_ref[1].astype(F32)).astype(BF)


def call(kernel, name, out_shape, scratch, flops, *args, there=()):
    many = isinstance(out_shape, tuple)
    vmem = pl.BlockSpec(memory_space=pltpu.VMEM)
    smem = pl.BlockSpec(memory_space=pltpu.SMEM)
    specs = [smem if a.dtype == jnp.int32 else vmem for a in args]
    for n in there:
        specs[n] = pl.BlockSpec(memory_space=pltpu.MemorySpace.HBM)
    return pl.pallas_call(
        kernel,
        name=name,
        out_shape=out_shape,
        in_specs=specs,
        out_specs=(vmem,) * len(out_shape) if many else vmem,
        scratch_shapes=scratch,
        compiler_params=pltpu.CompilerParams(vmem_limit_bytes=VMEM_LIMIT),
        cost_estimate=pl.CostEstimate(
            flops=flops, bytes_accessed=1 << 20, transcendentals=flops // 2560
        ),
    )(*args)


def take(x, axis, size, by):
    return lax.ppermute(x, axis, [((i + by) % size, i) for i in range(size)])


def swap(x, bit):
    return lax.ppermute(x, "h", [(i, i ^ bit) for i in range(HEADS)])


def gather(x):
    far = swap(x, 2)
    return [x, swap(x, 1), far, swap(far, 1)]


def after(x, *others):
    return lax.optimization_barrier((x,) + others)[0]


def heads_terms(a, w, transposed):
    size = ROWS // HEADS
    own, send = call(
        functools.partial(heads_kernel, transposed),
        "heads_terms",
        (jax.ShapeDtypeStruct((2, size, 1024), F32), jax.ShapeDtypeStruct((2, size, 1024), BF)),
        [],
        2 * FLOPS * ROWS * 1024 * a.shape[1],
        a,
        w,
    )
    return own, swap(send, 1)


def add_heads(own, got, *others):
    size = ROWS // HEADS
    keep, send = call(
        chip_kernel,
        "heads_sum",
        (jax.ShapeDtypeStruct((size, 1024), F32), jax.ShapeDtypeStruct((size, 1024), BF)),
        [],
        10**8,
        own,
        got,
    )
    return keep + swap(after(send, *others), 2).astype(F32)


def exchange(x, axis):
    return lax.all_to_all(x, axis, split_axis=0, concat_axis=0, tiled=True)


class Ring:
    def __init__(self, block):
        self.blocks = {0: [block]}
        self.steps = 0

    def step(self, *others):
        r = self.steps = self.steps + 1
        up, down = self.blocks[r - 1][0], self.blocks[(1 - r) % NZ][0]
        if r < NZ // 2:
            self.blocks[r] = [take(after(up, *others), "z", NZ, 1)]
            self.blocks[NZ - r] = [take(after(down, *others), "z", NZ, -1)]
        else:
            half = ROWS // 2
            self.blocks[r] = [
                take(after(up[:half], *others), "z", NZ, 1),
                take(after(down[half:], *others), "z", NZ, -1),
            ]

    def pieces(self, number):
        return [piece for d in number for piece in self.blocks[d]]


def spread(x, axis, size):
    return exchange(jnp.broadcast_to(x[None], (size,) + x.shape), axis)


def span_bias(block_mask, span_order, z, h):
    order = jnp.tile(span_order.reshape(NZ, 2, 2, 2), (2, 1, 1, 1))
    order = lax.dynamic_slice(order, (z, 0, 0, 0), (NZ, 2, 2, 2))
    order = jnp.where(h // 2 == 1, order[:, ::-1], order)
    order = jnp.where(h % 2 == 1, order[:, :, ::-1], order).reshape(64) // 2
    hot = (order[:, None] == jnp.arange(32, dtype=jnp.int32)[None, :]).astype(F32)
    linked = dot(dot(hot, block_mask.astype(F32)), hot.T)
    bias = jnp.where(linked > 0.5, 0.0, NEG).astype(F32)
    by_group = jnp.transpose(bias[:8].reshape(8, NZ, 8), (1, 0, 2)).reshape(64, 8)
    both = jnp.repeat(jnp.concatenate([by_group, bias[:8].T]), SPAN, axis=1)
    return both[:64, None, :], both[64:, None, :]


def body(tokens, cotangent, w_query, w_key, w_value, w_out, block_mask, span_order):
    x_own = tokens[0]
    dy_own = cotangent[0]
    h = lax.axis_index("h")
    z = lax.axis_index("z")
    bias_q, bias_b = span_bias(block_mask, span_order, z, h)

    def head(w):
        return lax.dynamic_slice(w, (0, h * HD), (w.shape[0], HD))

    work = FLOPS * ROWS * ROWS * HD
    head_rows = jax.ShapeDtypeStruct((ROWS, HD), BF)
    pair_rows = jax.ShapeDtypeStruct((ROWS, 2 * HD), BF)
    model_rows = jax.ShapeDtypeStruct((ROWS, 1024), BF)
    state_shape = (3, ROWS, HD)
    acc_shape = (HD, ROWS)

    def staging(groups, at_once, pieces):
        blocks = pltpu.VMEM((groups // at_once, at_once * ROWS, 2 * HD), BF)
        return [blocks, pltpu.SemaphoreType.DMA((pieces,))]

    x_near = gather(x_own)

    def half_of_head(turned):
        pairs = []
        for m in range(NF):
            for a in range(HEADS):
                clip = 2 * a + (m // 4) ^ turned
                pairs.append((clip * HEADS + m % 4, m * HEADS + a))
        return lax.ppermute(after(w_out, x_near[2]), ("f", "h"), pairs)

    halves = half_of_head(0), half_of_head(1)
    mine = jnp.concatenate([head(w_key), head(w_value), head(w_query)], axis=1)
    w_head = spread(mine, "f", NF).reshape(1024, 3 * HD)
    kv, q, x = call(
        tokens_kernel,
        "tokens",
        (pair_rows, head_rows, model_rows),
        [],
        3 * work,
        *x_near,
        after(w_head, bias_q, bias_b, *halves),
    )
    kv_ring = Ring(kv)
    kv_ring.step()
    dy_near = gather(after(dy_own, kv))
    g, dy, out_head = call(
        cotangent_kernel,
        "cotangent",
        (head_rows, model_rows, jax.ShapeDtypeStruct((HD, 1024), BF)),
        [],
        2 * work,
        lax.axis_index("f").reshape(1),
        *halves,
        *dy_near,
    )

    def forward(number, state, *more, q=q):
        at_once = 1
        pieces = kv_ring.pieces(number)
        last = bool(more)
        shape = jax.ShapeDtypeStruct(state_shape, F32)
        if last:
            shape = (
                head_rows,
                jax.ShapeDtypeStruct((2, ROWS), F32),
            )
        count = len(number)
        return call(
            functools.partial(forward_kernel, len(pieces), at_once, not state, last),
            "attn_forward_end" if last else "attn_forward",
            shape,
            ([pltpu.VMEM(state_shape, F32)] if last else []) + staging(count, at_once, len(pieces)),
            2 * work * count,
            jnp.array(number, jnp.int32),
            q,
            *pieces,
            bias_q,
            *state,
            *more,
            there=range(2, 2 + len(pieces)),
        )

    kv_ring.step()
    state = (forward((0, 1, 7), (), q=after(q, *dy_near)),)
    kv_ring.step(*state)
    state = (forward((2, 6), state),)
    kv_ring.step(*state)
    state = (forward((3, 5), state),)
    att, stat = forward((4,), state, g)

    def backward(number, acc, last=False):
        pieces = kv_ring.pieces(number)
        count = len(number)
        out = call(
            functools.partial(backward_kernel, len(pieces), not acc, last),
            "attn_backward",
            (
                jax.ShapeDtypeStruct((count, ROWS, 2 * HD), BF),
                head_rows if last else jax.ShapeDtypeStruct(acc_shape, F32),
            ),
            ([pltpu.VMEM(acc_shape, F32)] if last else []) + staging(count, 1, len(pieces)),
            5 * work * count,
            q,
            g,
            stat,
            jnp.array(number, jnp.int32),
            *pieces,
            bias_b,
            *acc,
            there=range(4, 4 + len(pieces)),
        )
        return out

    def add(part, got):
        return (part.astype(F32) + got.astype(F32)).astype(BF)

    half = ROWS // 2
    part, acc = backward((4,), ())
    up = take(part[0, :half], "z", NZ, -1)
    down = take(part[0, half:], "z", NZ, 1)
    part, acc = backward((3, 5), (acc,))
    up = jnp.concatenate([add(part[0, :half], up), part[0, half:]], axis=0)
    down = jnp.concatenate([part[1, :half], add(part[1, half:], down)], axis=0)
    up, down = take(up, "z", NZ, -1), take(down, "z", NZ, 1)
    mixed = heads_terms(after(att, acc), out_head, False)
    part, acc = backward((2, 6), (acc,))
    up, down = add(part[0], up), add(part[1], down)
    part, dq = backward((1, 7, 0), (after(acc, up, down),), last=True)
    up, down = take(up, "z", NZ, -1), take(down, "z", NZ, 1)
    up, down = add(part[0], up), add(part[1], down)
    up, down = take(up, "z", NZ, -1), take(down, "z", NZ, 1)

    mixed = (x_own.astype(F32) + add_heads(*mixed)).astype(BF)
    grad_o = call(
        out_kernel,
        "grad_out",
        jax.ShapeDtypeStruct((NF, HD, HD), BF),
        [
            pltpu.VMEM((HEADS * ROWS, HD), BF),
            pltpu.VMEM((ROWS, 256), BF),
            pltpu.SemaphoreType.DMA((HEADS,)),
            pltpu.SemaphoreType.DMA,
        ],
        2 * work,
        h.reshape(1),
        *gather(att),
        dy,
        there=range(1, HEADS + 2),
    )
    grad_q = dot_tn(x, dq).astype(BF).reshape(NF, HD, HD)

    own = after(part[2], grad_q, grad_o, mixed)
    dkv = (own.astype(F32) + up.astype(F32) + down.astype(F32)).astype(BF)

    grad_kv = dot_tn(x, dkv).astype(BF).reshape(NF, HD, 2 * HD)
    terms = jnp.concatenate([grad_q, grad_kv, grad_o], axis=2)
    got = jnp.sum(exchange(terms, "f").astype(F32), axis=0).astype(BF)
    got_o = jnp.transpose(got[:, 3 * HD :].reshape(2, 32, 2, HD), (1, 0, 2, 3)).reshape(32, 4, HD)
    got = jnp.concatenate([got[:, : 3 * HD].reshape(32, 4, 3 * HD), got_o], axis=2)
    d_head = jnp.concatenate([after(dkv, terms), dq], axis=1)
    token_grad = heads_terms(d_head, w_head, True)
    token_grad = (dy_own.astype(F32) + add_heads(*token_grad, got)).astype(BF)

    sums = after(exchange(got, ("z", "h")), token_grad).reshape(NZ, HEADS, 4, 4 * HD)
    sums = jnp.sum(sums.astype(F32), axis=0)
    grads = sums[:, :, : 3 * HD].reshape(HEADS, 4, 3, HD)
    grads = jnp.transpose(grads, (2, 1, 0, 3)).reshape(3, 4, HEADS * HD)
    grad_o = sums[:, :, 3 * HD :].reshape(HEADS, 2, 2, HD)
    grad_o = jnp.transpose(grad_o, (2, 0, 1, 3)).reshape(2, 1024)
    return (mixed[None], token_grad[None], grads[0], grads[1], grads[2], grad_o)


def solution(mesh):
    fine = Mesh(mesh.devices.reshape(NF, NZ, HEADS), ("f", "z", "h"))
    rows = P("f", ("z", "h"), None)
    split = P(("f", "z", "h"), None)
    return jax.shard_map(
        body,
        mesh=fine,
        in_specs=(rows, rows, P("f", None), P("f", None), P("f", None), P("f", None), P(), P()),
        out_specs=(rows, rows, split, split, split, split),
        check_vma=False,
    )
```

profile of v0, /device:TPU:1, one launch (start us, length us, event | category | flops | bytes accessed | tf_op | source)
XLA Modules:
  0.0 152.0 jit_solution(15066615658812718400)
XLA Ops:
  0.6 2.1 %collective-permute-start.1 = (bf16[128,1024]{1,0:T(8,128)(2,1)}, bf16[128,1024]{1,0:T(8,128)(2,1)S(1)}, u32[]{:S(2)}, u32[]{:S(2)}) collective-permute-start(bf16[128,1024]{1,0:T(8,128)(2,1)} %bitcast.75), channel_id=1, source_target_pairs={{0,2},{1,3},{2,0},{3,1},{4,6},{5,7},{6,4},{7,5},{8,10},{9,11},{10,... | collective-permute-start | bytes 786440 | tf_op jit(solution)/shard_map/ppermute | solution.py:263
  2.8 1.3 collective-permute-start
  4.1 0.8 constant_dynamic-slice_fusion.1
  4.9 1.0 broadcast_in_dim.33
  5.9 6.1 %all-to-all-start = ((bf16[8,128,384]{2,1,0:T(8,128)(2,1)}), bf16[8,128,384]{2,1,0:T(8,128)(2,1)S(1)}, u32[]{:S(2)}, u32[]{:S(2)}) async-start(bf16[8,128,384]{2,1,0:T(8,128)(2,1)} %broadcast_in_dim.33), calls=%async_computation | async-start | bytes 1572864 | tf_op jit(solution)/shard_map/all_to_all | solution.py:304
  13.5 3.5 %collective-permute-start.3 = (bf16[64,1024]{1,0:T(8,128)(2,1)S(1)}, bf16[64,1024]{1,0:T(8,128)(2,1)S(1)}, u32[]{:S(2)}, u32[]{:S(2)}) collective-permute-start(bf16[64,1024]{1,0:T(8,128)(2,1)S(1)} %copy-done.29), channel_id=1, source_target_pairs={{0,0},{64,1},{128,2},{192,3},{1,32},{65,33},{129,34},{193,35},{2,6... | collective-permute-start | bytes 393224 | tf_op jit(solution)/shard_map/ppermute | solution.py:375
  17.0 3.3 %collective-permute-start.4 = (bf16[64,1024]{1,0:T(8,128)(2,1)S(1)}, bf16[64,1024]{1,0:T(8,128)(2,1)S(1)}, u32[]{:S(2)}, u32[]{:S(2)}) collective-permute-start(bf16[64,1024]{1,0:T(8,128)(2,1)S(1)} %copy-done.29), channel_id=1, source_target_pairs={{32,0},{96,1},{160,2},{224,3},{33,32},{97,33},{161,34},{225,35},{3... | collective-permute-start | bytes 393224 | tf_op jit(solution)/shard_map/ppermute | solution.py:375
  21.2 6.3 %collective-permute-done.3.a_ref = bf16[64,1024]{1,0:T(8,128)(2,1)S(1)} collective-permute-done((bf16[64,1024]{1,0:T(8,128)(2,1)S(1)}, bf16[64,1024]{1,0:T(8,128)(2,1)S(1)}, u32[]{:S(2)}, u32[]{:S(2)}) %collective-permute-start.3) | collective-permute-done | bytes 131104 | tf_op jit(solution)/shard_map/ppermute | solution.py:375
  27.5 0.7 copy-done.15
  28.1 0.6 copy-done.17
  28.8 0.7 copy-done.13
  29.5 0.9 copy-done.14
  30.4 0.7 tokens.1
  31.2 5.4 %collective-permute-start.8 = (bf16[128,1024]{1,0:T(8,128)(2,1)S(1)}, bf16[128,1024]{1,0:T(8,128)(2,1)S(1)}, u32[]{:S(2)}, u32[]{:S(2)}) collective-permute-start(bf16[128,1024]{1,0:T(8,128)(2,1)S(1)} %bitcast.78), channel_id=1, source_target_pairs={{0,2},{1,3},{2,0},{3,1},{4,6},{5,7},{6,4},{7,5},{8,10},{9,11},{10,... | collective-permute-start | bytes 786440 | tf_op jit(solution)/shard_map/ppermute | solution.py:263
  36.5 1.6 %collective-permute-start.10 = (bf16[512,256]{1,0:T(8,128)(2,1)S(1)}, bf16[512,256]{1,0:T(8,128)(2,1)S(1)}, u32[]{:S(2)}, u32[]{:S(2)}) collective-permute-start(bf16[512,256]{1,0:T(8,128)(2,1)S(1)} %get-tuple-element.47.refs_1_.refs_2_), channel_id=1, source_target_pairs={{28,0},{0,4},{4,8},{8,12},{12,16},{16,20},{20,24},{24,28},{29,1},{... | collective-permute-start | bytes 786440 | tf_op jit(solution)/shard_map/ppermute | solution.py:259
  38.2 3.9 %collective-permute-start.5 = (bf16[512,256]{1,0:T(8,128)(2,1)S(1)}, bf16[512,256]{1,0:T(8,128)(2,1)S(1)}, u32[]{:S(2)}, u32[]{:S(2)}) collective-permute-start(bf16[512,256]{1,0:T(8,128)(2,1)S(1)} %get-tuple-element.47.refs_1_.refs_2_), channel_id=1, source_target_pairs={{4,0},{8,4},{12,8},{16,12},{20,16},{24,20},{28,24},{0,28},{5,1},{9... | collective-permute-start | bytes 786440 | tf_op jit(solution)/shard_map/ppermute | solution.py:259
  42.6 4.9 %collective-permute-done.10.refs_3_.refs_1_ = bf16[512,256]{1,0:T(8,128)(2,1)S(1)} collective-permute-done((bf16[512,256]{1,0:T(8,128)(2,1)S(1)}, bf16[512,256]{1,0:T(8,128)(2,1)S(1)}, u32[]{:S(2)}, u32[]{:S(2)}) %collective-permute-start.10) | collective-permute-done | bytes 262176 | tf_op jit(solution)/shard_map/ppermute | solution.py:259
  47.5 2.9 %collective-permute-start.6 = (bf16[512,256]{1,0:T(8,128)(2,1)S(1)}, bf16[512,256]{1,0:T(8,128)(2,1)}, u32[]{:S(2)}, u32[]{:S(2)}) collective-permute-start(bf16[512,256]{1,0:T(8,128)(2,1)S(1)} %collective-permute-done.5.refs_2_.refs_0_), channel_id=1, source_target_pairs={{4,0},{8,4},{12,8},{16,12},{20,16},{24,20},{28,24},{0,28},{5,1},{9... | collective-permute-start | bytes 786440 | tf_op jit(solution)/shard_map/ppermute | solution.py:259
  50.5 0.7 copy-done.9
  51.2 0.7 copy-done.11
  51.9 2.4 %attn_forward.3.refs_4_ = f32[3,512,128]{2,1,0:T(8,128)S(1)} custom-call(s32[3]{0:T(128)S(1)} %copy-done.22, bf16[512,128]{1,0:T(8,128)(2,1)S(1)} %get-tuple-element.49.refs_0_.q_ref, bf16[512,256]{1,0:T(8,128)(2,1)S(1)} %get-tuple-element.47.refs_1_.refs_2_, bf16[512,256]{1,0:T(8,128)(2,1)S(1)} %collective-permute-done.5.refs_2_.refs_0_, ...), custom_call_target="tpu_custom_call" | custom-call | flops 1610612736 | bytes 1048576 | tf_op jit(solution)/shard_map/attn_forward/pallas_call | solution.py:244
  54.4 0.6 copy-done.23
  55.0 0.9 copy-done.26
  56.0 1.2 collective-permute-done.12.refs_2_.refs_1_
  57.1 2.7 %collective-permute-start.11 = (bf16[512,256]{1,0:T(8,128)(2,1)}, bf16[512,256]{1,0:T(8,128)(2,1)S(1)}, u32[]{:S(2)}, u32[]{:S(2)}) collective-permute-start(bf16[512,256]{1,0:T(8,128)(2,1)} %collective-permute-done.6.refs_1_.refs_0_), channel_id=1, source_target_pairs={{4,0},{8,4},{12,8},{16,12},{20,16},{24,20},{28,24},{0,28},{5,1},{9... | collective-permute-start | bytes 786440 | tf_op jit(solution)/shard_map/ppermute | solution.py:259
  59.8 0.9 copy-done.24
  60.7 1.1 copy-done.27
  61.9 2.7 %attn_forward.4.refs_4_ = f32[3,512,128]{2,1,0:T(8,128)S(1)} custom-call(s32[2]{0:T(128)S(1)} %copy-done.20, bf16[512,128]{1,0:T(8,128)(2,1)S(1)} %copy-done.24, bf16[512,256]{1,0:T(8,128)(2,1)} %collective-permute-done.6.refs_1_.refs_0_, bf16[512,256]{1,0:T(8,128)(2,1)} %collective-permute-done.12.refs_2_.refs_1_, ...), custom_call_target="tpu_custom_call" | custom-call | flops 1073741824 | bytes 1048576 | tf_op jit(solution)/shard_map/attn_forward/pallas_call | solution.py:244
  64.6 1.5 collective-permute-done.14.refs_2_.refs_1_
  66.4 2.7 %collective-permute-start.13 = (bf16[256,256]{1,0:T(8,128)(2,1)S(1)}, bf16[256,256]{1,0:T(8,128)(2,1)S(1)}, u32[]{:S(2)}, u32[]{:S(2)}) collective-permute-start(bf16[256,256]{1,0:T(8,128)(2,1)S(1)} %slice.95), channel_id=1, source_target_pairs={{4,0},{8,4},{12,8},{16,12},{20,16},{24,20},{28,24},{0,28},{5,1},{9... | collective-permute-start | bytes 393224 | tf_op jit(solution)/shard_map/ppermute | solution.py:259
  69.7 1.9 %attn_forward.5.refs_4_ = f32[3,512,128]{2,1,0:T(8,128)S(1)} custom-call(s32[2]{0:T(128)S(1)} %copy-done.21, bf16[512,128]{1,0:T(8,128)(2,1)S(1)} %copy-done.25, bf16[512,256]{1,0:T(8,128)(2,1)S(1)} %collective-permute-done.11.refs_1_.refs_0_, bf16[512,256]{1,0:T(8,128)(2,1)S(1)} %collective-permute-done.14.refs_2_.refs_1_, ...), custom_call_target="tpu_custom_call" | custom-call | flops 1073741824 | bytes 1048576 | tf_op jit(solution)/shard_map/attn_forward/pallas_call | solution.py:244
  71.6 1.3 attn_forward_end.1
  73.0 2.3 %collective-permute-start.22 = (bf16[512,128]{1,0:T(8,128)(2,1)S(1)}, bf16[512,128]{1,0:T(8,128)(2,1)S(1)}, u32[]{:S(2)}, u32[]{:S(2)}) collective-permute-start(bf16[512,128]{1,0:T(8,128)(2,1)S(1)} %get-tuple-element.59.a_ref.refs_0_), channel_id=1, source_target_pairs={{0,1},{1,0},{2,3},{3,2},{4,5},{5,4},{6,7},{7,6},{8,9},{9,8},{10,11... | collective-permute-start | bytes 393224 | tf_op jit(solution)/shard_map/ppermute | solution.py:263
  75.2 1.1 attn_backward.4
  76.5 3.1 %collective-permute-start.20 = (bf16[256,256]{1,0:T(8,128)(2,1)S(1)}, bf16[256,256]{1,0:T(8,128)(2,1)S(1)}, u32[]{:S(2)}, u32[]{:S(2)}) collective-permute-start(bf16[256,256]{1,0:T(8,128)(2,1)S(1)} %get-tuple-element.90), channel_id=1, source_target_pairs={{4,0},{8,4},{12,8},{16,12},{20,16},{24,20},{28,24},{0,28},{5,1},{9... | collective-permute-start | bytes 393224 | tf_op jit(solution)/shard_map/ppermute | solution.py:259
  79.6 2.2 %attn_backward.5 = (bf16[2,512,256]{2,1,0:T(8,128)(2,1)S(1)}, f32[128,512]{1,0:T(8,128)S(1)}) custom-call(bf16[512,128]{1,0:T(8,128)(2,1)S(1)} %copy-done.25, bf16[512,128]{1,0:T(8,128)(2,1)S(1)} %get-tuple-element.54.refs_5_.g_ref, f32[2,512]{1,0:T(2,128)S(1)} %get-tuple-element.56.stat_ref, s32[2]{0:T(128)S(1)} %copy-done.21, ...), custom_call_target="tpu_custom_call" | custom-call | flops 2684354560 | bytes 1048576 | tf_op jit(solution)/shard_map/attn_backward/pallas_call | solution.py:244
  82.7 0.7 collective-permute-done.18
  83.4 2.4 %collective-permute-start.19 = (bf16[512,256]{1,0:T(8,128)(2,1)S(1)}, bf16[512,256]{1,0:T(8,128)(2,1)S(1)}, u32[]{:S(2)}, u32[]{:S(2)}) collective-permute-start(bf16[512,256]{1,0:T(8,128)(2,1)S(1)} %pad_maximum_fusion.2), channel_id=1, source_target_pairs={{28,0},{0,4},{4,8},{8,12},{12,16},{16,20},{20,24},{24,28},{29,1},{... | collective-permute-start | bytes 786440 | tf_op jit(solution)/shard_map/ppermute | solution.py:259
  86.3 1.2 collective-permute-start.24
  87.5 3.1 %attn_backward.6 = (bf16[2,512,256]{2,1,0:T(8,128)(2,1)S(1)}, f32[128,512]{1,0:T(8,128)S(1)}) custom-call(bf16[512,128]{1,0:T(8,128)(2,1)S(1)} %copy-done.25, bf16[512,128]{1,0:T(8,128)(2,1)S(1)} %get-tuple-element.54.refs_5_.g_ref, f32[2,512]{1,0:T(2,128)S(1)} %get-tuple-element.56.stat_ref, s32[2]{0:T(128)S(1)} %copy-done.20, ...), custom_call_target="tpu_custom_call" | custom-call | flops 2684354560 | bytes 1048576 | tf_op jit(solution)/shard_map/attn_backward/pallas_call | solution.py:244
  90.6 1.7 %grad_out.1 = bf16[8,128,128]{2,1,0:T(8,128)(2,1)S(1)} custom-call(s32[1]{0:T(128)} %bitcast.18.h_ref, bf16[512,128]{1,0:T(8,128)(2,1)S(1)} %get-tuple-element.59.a_ref.refs_0_, bf16[512,128]{1,0:T(8,128)(2,1)S(1)} %collective-permute-done.22.refs_1_, bf16[512,128]{1,0:T(8,128)(2,1)S(1)} %collective-permute-done.23.refs_2_, ...), custom_call_target="tpu_custom_call" | custom-call | flops 536870912 | bytes 1048576 | tf_op jit(solution)/shard_map/grad_out/pallas_call | solution.py:244
  92.8 1.2 collective-permute-start.25
  94.0 1.5 %collective-permute-start.27 = (bf16[512,256]{1,0:T(8,128)(2,1)S(1)}, bf16[512,256]{1,0:T(8,128)(2,1)S(1)}, u32[]{:S(2)}, u32[]{:S(2)}) collective-permute-start(bf16[512,256]{1,0:T(8,128)(2,1)S(1)} %get-tuple-element.84), channel_id=1, source_target_pairs={{4,0},{8,4},{12,8},{16,12},{20,16},{24,20},{28,24},{0,28},{5,1},{9... | collective-permute-start | bytes 786440 | tf_op jit(solution)/shard_map/ppermute | solution.py:259
  95.5 3.1 %attn_backward.7 = (bf16[3,512,256]{2,1,0:T(8,128)(2,1)S(1)}, bf16[512,128]{1,0:T(8,128)(2,1)S(1)}) custom-call(bf16[512,128]{1,0:T(8,128)(2,1)S(1)} %copy-done.25, bf16[512,128]{1,0:T(8,128)(2,1)S(1)} %get-tuple-element.54.refs_5_.g_ref, f32[2,512]{1,0:T(2,128)S(1)} %get-tuple-element.56.stat_ref, s32[3]{0:T(128)S(1)} %copy-done.19, ...), custom_call_target="tpu_custom_call" | custom-call | flops 4026531840 | bytes 1048576 | tf_op jit(solution)/shard_map/attn_backward/pallas_call | solution.py:244
  99.3 1.5 collective-permute-start.17
  100.9 0.6 collective-permute-start.26
  101.5 2.1 %collective-permute-start.28 = (bf16[512,256]{1,0:T(8,128)(2,1)S(1)}, bf16[512,256]{1,0:T(8,128)(2,1)S(1)}, u32[]{:S(2)}, u32[]{:S(2)}) collective-permute-start(bf16[512,256]{1,0:T(8,128)(2,1)S(1)} %get-tuple-element.83), channel_id=1, source_target_pairs={{4,0},{8,4},{12,8},{16,12},{20,16},{24,20},{28,24},{0,28},{5,1},{9... | collective-permute-start | bytes 786440 | tf_op jit(solution)/shard_map/ppermute | solution.py:259
  103.7 0.9 collective-permute-done.17
  104.6 0.8 add_convert_fusion.2
  105.4 2.1 %collective-permute-done.26 = bf16[512,256]{1,0:T(8,128)(2,1)S(1)} collective-permute-done((bf16[512,256]{1,0:T(8,128)(2,1)S(1)}, bf16[512,256]{1,0:T(8,128)(2,1)S(1)}, u32[]{:S(2)}, u32[]{:S(2)}) %collective-permute-start.26) | collective-permute-done | bytes 262176 | tf_op jit(solution)/shard_map/ppermute | solution.py:259
  108.0 1.1 pad_maximum_fusion
  109.1 4.2 %all-to-all-start.1 = ((bf16[8,128,512]{2,1,0:T(8,128)(2,1)}), bf16[8,128,512]{2,1,0:T(8,128)(2,1)}, u32[]{:S(2)}, u32[]{:S(2)}) async-start(bf16[8,128,512]{2,1,0:T(8,128)(2,1)} %pad_maximum_fusion), calls=%async_computation.1 | async-start | bytes 2097152 | tf_op jit(solution)/shard_map/all_to_all | solution.py:304
  113.4 0.7 heads_terms.3
  114.2 4.0 %collective-permute-start.29 = (bf16[2,128,1024]{2,1,0:T(8,128)(2,1)S(1)}, bf16[2,128,1024]{2,1,0:T(8,128)(2,1)S(1)}, u32[]{:S(2)}, u32[]{:S(2)}) collective-permute-start(bf16[2,128,1024]{2,1,0:T(8,128)(2,1)S(1)} %get-tuple-element.77), channel_id=1, source_target_pairs={{0,1},{1,0},{2,3},{3,2},{4,5},{5,4},{6,7},{7,6},{8,9},{9,8},{10,11... | collective-permute-start | bytes 1572872 | tf_op jit(solution)/shard_map/ppermute | solution.py:263
  118.2 1.5 %collective-permute-done.29.got_ref = bf16[2,128,1024]{2,1,0:T(8,128)(2,1)S(1)} collective-permute-done((bf16[2,128,1024]{2,1,0:T(8,128)(2,1)S(1)}, bf16[2,128,1024]{2,1,0:T(8,128)(2,1)S(1)}, u32[]{:S(2)}, u32[]{:S(2)}) %collective-permute-start.29) | collective-permute-done | bytes 524320 | tf_op jit(solution)/shard_map/ppermute | solution.py:263
  119.9 4.7 %all-to-all-done.1 = bf16[8,128,512]{2,1,0:T(8,128)(2,1)} async-done(((bf16[8,128,512]{2,1,0:T(8,128)(2,1)}), bf16[8,128,512]{2,1,0:T(8,128)(2,1)}, u32[]{:S(2)}, u32[]{:S(2)}) %all-to-all-start.1) | async-done | bytes 1048608 | tf_op jit(solution)/shard_map/all_to_all | solution.py:304
  124.5 1.4 reduce_sum.21
  126.0 0.7 constant_dynamic-update-slice_fusion
  126.7 0.6 copy_dynamic-update-slice_fusion
  127.3 1.8 %collective-permute-start.30 = (bf16[128,1024]{1,0:T(8,128)(2,1)S(1)}, bf16[128,1024]{1,0:T(8,128)(2,1)S(1)}, u32[]{:S(2)}, u32[]{:S(2)}) collective-permute-start(bf16[128,1024]{1,0:T(8,128)(2,1)S(1)} %get-tuple-element.80), channel_id=1, source_target_pairs={{0,2},{1,3},{2,0},{3,1},{4,6},{5,7},{6,4},{7,5},{8,10},{9,11},{10,... | collective-permute-start | bytes 786440 | tf_op jit(solution)/shard_map/ppermute | solution.py:263
  129.1 12.4 %all-to-all-start.2 = ((bf16[32,4,512]{2,1,0:T(4,128)(2,1)}), bf16[32,4,512]{2,1,0:T(4,128)(2,1)S(1)}, u32[]{:S(2)}, u32[]{:S(2)}) async-start(bf16[32,4,512]{2,1,0:T(4,128)(2,1)} %copy_dynamic-update-slice_fusion), calls=%async_computation.2 | async-start | bytes 262144 | tf_op jit(solution)/shard_map/all_to_all | solution.py:304
  141.5 0.8 add_convert_fusion
  142.3 8.4 %all-to-all-done.2 = bf16[32,4,512]{2,1,0:T(4,128)(2,1)S(1)} async-done(((bf16[32,4,512]{2,1,0:T(4,128)(2,1)}), bf16[32,4,512]{2,1,0:T(4,128)(2,1)S(1)}, u32[]{:S(2)}, u32[]{:S(2)}) %all-to-all-start.2) | async-done | bytes 131104 | tf_op jit(solution)/shard_map/all_to_all | solution.py:304
  151.4 0.6 slice_bitcast_fusion.6
  (132 shorter events, 7.8 us)
Async XLA Ops:
  0.6 3.4 %copy-start = (bf16[128,512]{1,0:T(8,128)(2,1)S(1)}, bf16[128,512]{1,0:T(8,128)(2,1)}, u32[]{:S(2)}) copy-start(bf16[128,512]{1,0:T(8,128)(2,1)} %param.19) | copy-start | bytes 393220
  0.6 12.1 %collective-permute-start.1 = (bf16[128,1024]{1,0:T(8,128)(2,1)}, bf16[128,1024]{1,0:T(8,128)(2,1)S(1)}, u32[]{:S(2)}, u32[]{:S(2)}) collective-permute-start(bf16[128,1024]{1,0:T(8,128)(2,1)} %bitcast.75), channel_id=1, source_target_pairs={{0,2},{1,3},{2,0},{3,1},{4,6},{5,7},{6,4},{7,5},{8,10},{9,11},{10,... | collective-permute-start | bytes 786440 | tf_op jit(solution)/shard_map/ppermute | solution.py:263
  2.8 26.0 %collective-permute-start = (bf16[128,1024]{1,0:T(8,128)(2,1)}, bf16[128,1024]{1,0:T(8,128)(2,1)S(1)}, u32[]{:S(2)}, u32[]{:S(2)}) collective-permute-start(bf16[128,1024]{1,0:T(8,128)(2,1)} %bitcast.76), channel_id=1, source_target_pairs={{0,1},{1,0},{2,3},{3,2},{4,5},{5,4},{6,7},{7,6},{8,9},{9,8},{10,11... | collective-permute-start | bytes 786440 | tf_op jit(solution)/shard_map/ppermute | solution.py:263
  4.9 7.2 %copy-start.28 = (s32[64]{0:T(128)S(1)}, s32[64]{0:T(128)}, u32[]{:S(2)}) copy-start(s32[64]{0:T(128)} %param.23) | copy-start | bytes 772
  5.9 7.2 %copy-start.30 = (s32[32,32]{1,0:T(8,128)S(1)}, s32[32,32]{1,0:T(8,128)}, u32[]{:S(2)}) copy-start(s32[32,32]{1,0:T(8,128)} %param.22) | copy-start | bytes 12292
  5.9 7.6 %copy-start.29 = (bf16[64,1024]{1,0:T(8,128)(2,1)S(1)}, bf16[64,1024]{1,0:T(8,128)(2,1)}, u32[]{:S(2)}) copy-start(bf16[64,1024]{1,0:T(8,128)(2,1)} %param.21) | copy-start | bytes 393220
  5.9 22.9 %all-to-all-start = ((bf16[8,128,384]{2,1,0:T(8,128)(2,1)}), bf16[8,128,384]{2,1,0:T(8,128)(2,1)S(1)}, u32[]{:S(2)}, u32[]{:S(2)}) async-start(bf16[8,128,384]{2,1,0:T(8,128)(2,1)} %broadcast_in_dim.33), calls=%async_computation | async-start | bytes 1572864 | tf_op jit(solution)/shard_map/all_to_all | solution.py:304
  12.1 17.4 %copy-start.1 = (bf16[1,128,1024]{2,1,0:T(8,128)(2,1)S(1)}, bf16[1,128,1024]{2,1,0:T(8,128)(2,1)}, u32[]{:S(2)}) copy-start(bf16[1,128,1024]{2,1,0:T(8,128)(2,1)} %param.16) | copy-start | bytes 786436
  12.8 16.0 %collective-permute-start.2 = (bf16[128,1024]{1,0:T(8,128)(2,1)S(1)}, bf16[128,1024]{1,0:T(8,128)(2,1)S(1)}, u32[]{:S(2)}, u32[]{:S(2)}) collective-permute-start(bf16[128,1024]{1,0:T(8,128)(2,1)S(1)} %collective-permute-done.1.refs_2_), channel_id=1, source_target_pairs={{0,1},{1,0},{2,3},{3,2},{4,5},{5,4},{6,7},{7,6},{8,9},{9,8},{10,11... | collective-permute-start | bytes 786440 | tf_op jit(solution)/shard_map/ppermute | solution.py:263
  13.5 13.9 %collective-permute-start.3 = (bf16[64,1024]{1,0:T(8,128)(2,1)S(1)}, bf16[64,1024]{1,0:T(8,128)(2,1)S(1)}, u32[]{:S(2)}, u32[]{:S(2)}) collective-permute-start(bf16[64,1024]{1,0:T(8,128)(2,1)S(1)} %copy-done.29), channel_id=1, source_target_pairs={{0,0},{64,1},{128,2},{192,3},{1,32},{65,33},{129,34},{193,35},{2,6... | collective-permute-start | bytes 393224 | tf_op jit(solution)/shard_map/ppermute | solution.py:375
  17.0 11.1 %collective-permute-start.4 = (bf16[64,1024]{1,0:T(8,128)(2,1)S(1)}, bf16[64,1024]{1,0:T(8,128)(2,1)S(1)}, u32[]{:S(2)}, u32[]{:S(2)}) collective-permute-start(bf16[64,1024]{1,0:T(8,128)(2,1)S(1)} %copy-done.29), channel_id=1, source_target_pairs={{32,0},{96,1},{160,2},{224,3},{33,32},{97,33},{161,34},{225,35},{3... | collective-permute-start | bytes 393224 | tf_op jit(solution)/shard_map/ppermute | solution.py:375
  27.5 0.7 copy-start.15
  28.8 23.1 %copy-start.22 = (s32[3]{0:T(128)S(1)}, s32[3]{0:T(128)}, u32[]{:S(2)}) copy-start(s32[3]{0:T(128)} %constant.72.clone.number_ref) | copy-start | bytes 40
  28.8 2.4 %copy-start.2 = (bf16[1,128,1024]{2,1,0:T(8,128)(2,1)S(1)}, bf16[1,128,1024]{2,1,0:T(8,128)(2,1)}, u32[]{:S(2)}) copy-start(bf16[1,128,1024]{2,1,0:T(8,128)(2,1)} %param.17) | copy-start | bytes 786436
  28.8 0.7 copy-start.13
  29.5 1.0 copy-start.14
  31.2 10.9 %collective-permute-start.8 = (bf16[128,1024]{1,0:T(8,128)(2,1)S(1)}, bf16[128,1024]{1,0:T(8,128)(2,1)S(1)}, u32[]{:S(2)}, u32[]{:S(2)}) collective-permute-start(bf16[128,1024]{1,0:T(8,128)(2,1)S(1)} %bitcast.78), channel_id=1, source_target_pairs={{0,2},{1,3},{2,0},{3,1},{4,6},{5,7},{6,4},{7,5},{8,10},{9,11},{10,... | collective-permute-start | bytes 786440 | tf_op jit(solution)/shard_map/ppermute | solution.py:263
  36.5 11.0 %collective-permute-start.10 = (bf16[512,256]{1,0:T(8,128)(2,1)S(1)}, bf16[512,256]{1,0:T(8,128)(2,1)S(1)}, u32[]{:S(2)}, u32[]{:S(2)}) collective-permute-start(bf16[512,256]{1,0:T(8,128)(2,1)S(1)} %get-tuple-element.47.refs_1_.refs_2_), channel_id=1, source_target_pairs={{28,0},{0,4},{4,8},{8,12},{12,16},{16,20},{20,24},{24,28},{29,1},{... | collective-permute-start | bytes 786440 | tf_op jit(solution)/shard_map/ppermute | solution.py:259
  38.2 9.4 %collective-permute-start.5 = (bf16[512,256]{1,0:T(8,128)(2,1)S(1)}, bf16[512,256]{1,0:T(8,128)(2,1)S(1)}, u32[]{:S(2)}, u32[]{:S(2)}) collective-permute-start(bf16[512,256]{1,0:T(8,128)(2,1)S(1)} %get-tuple-element.47.refs_1_.refs_2_), channel_id=1, source_target_pairs={{4,0},{8,4},{12,8},{16,12},{20,16},{24,20},{28,24},{0,28},{5,1},{9... | collective-permute-start | bytes 786440 | tf_op jit(solution)/shard_map/ppermute | solution.py:259
  42.1 8.4 %collective-permute-start.7 = (bf16[128,1024]{1,0:T(8,128)(2,1)S(1)}, bf16[128,1024]{1,0:T(8,128)(2,1)S(1)}, u32[]{:S(2)}, u32[]{:S(2)}) collective-permute-start(bf16[128,1024]{1,0:T(8,128)(2,1)S(1)} %bitcast.79), channel_id=1, source_target_pairs={{0,1},{1,0},{2,3},{3,2},{4,5},{5,4},{6,7},{7,6},{8,9},{9,8},{10,11... | collective-permute-start | bytes 786440 | tf_op jit(solution)/shard_map/ppermute | solution.py:263
  42.1 12.2 %copy-start.7 = (bf16[128,1024]{1,0:T(8,128)(2,1)}, bf16[128,1024]{1,0:T(8,128)(2,1)S(1)}, u32[]{:S(2)}) copy-start(bf16[128,1024]{1,0:T(8,128)(2,1)S(1)} %collective-permute-done.8.refs_2_) | copy-start | bytes 786436
  42.1 9.1 %collective-permute-start.9 = (bf16[128,1024]{1,0:T(8,128)(2,1)S(1)}, bf16[128,1024]{1,0:T(8,128)(2,1)S(1)}, u32[]{:S(2)}, u32[]{:S(2)}) collective-permute-start(bf16[128,1024]{1,0:T(8,128)(2,1)S(1)} %collective-permute-done.8.refs_2_), channel_id=1, source_target_pairs={{0,1},{1,0},{2,3},{3,2},{4,5},{5,4},{6,7},{7,6},{8,9},{9,8},{10,11... | collective-permute-start | bytes 786440 | tf_op jit(solution)/shard_map/ppermute | solution.py:263
  47.5 6.8 %copy-start.3 = (bf16[512,256]{1,0:T(8,128)(2,1)}, bf16[512,256]{1,0:T(8,128)(2,1)S(1)}, u32[]{:S(2)}) copy-start(bf16[512,256]{1,0:T(8,128)(2,1)S(1)} %collective-permute-done.10.refs_3_.refs_1_) | copy-start | bytes 786436
  47.5 9.6 %collective-permute-start.12 = (bf16[512,256]{1,0:T(8,128)(2,1)S(1)}, bf16[512,256]{1,0:T(8,128)(2,1)}, u32[]{:S(2)}, u32[]{:S(2)}) collective-permute-start(bf16[512,256]{1,0:T(8,128)(2,1)S(1)} %collective-permute-done.10.refs_3_.refs_1_), channel_id=1, source_target_pairs={{28,0},{0,4},{4,8},{8,12},{12,16},{16,20},{20,24},{24,28},{29,1},{... | collective-permute-start | bytes 786440 | tf_op jit(solution)/shard_map/ppermute | solution.py:259
  47.5 6.8 %copy-start.5 = (bf16[512,256]{1,0:T(8,128)(2,1)}, bf16[512,256]{1,0:T(8,128)(2,1)S(1)}, u32[]{:S(2)}) copy-start(bf16[512,256]{1,0:T(8,128)(2,1)S(1)} %collective-permute-done.5.refs_2_.refs_0_) | copy-start | bytes 786436
  47.5 9.6 %collective-permute-start.6 = (bf16[512,256]{1,0:T(8,128)(2,1)S(1)}, bf16[512,256]{1,0:T(8,128)(2,1)}, u32[]{:S(2)}, u32[]{:S(2)}) collective-permute-start(bf16[512,256]{1,0:T(8,128)(2,1)S(1)} %collective-permute-done.5.refs_2_.refs_0_), channel_id=1, source_target_pairs={{4,0},{8,4},{12,8},{16,12},{20,16},{24,20},{28,24},{0,28},{5,1},{9... | collective-permute-start | bytes 786440 | tf_op jit(solution)/shard_map/ppermute | solution.py:259
  50.5 0.7 copy-start.9
  51.2 0.7 copy-start.11
  51.9 7.9 %copy-start.20 = (s32[2]{0:T(128)S(1)}, s32[2]{0:T(128)}, u32[]{:S(2)}) copy-start(s32[2]{0:T(128)} %constant.73.clone.number_ref) | copy-start | bytes 28
  54.4 0.6 copy-start.23
  55.0 0.9 copy-start.26
  57.1 8.9 %collective-permute-start.14 = (bf16[512,256]{1,0:T(8,128)(2,1)}, bf16[512,256]{1,0:T(8,128)(2,1)S(1)}, u32[]{:S(2)}, u32[]{:S(2)}) collective-permute-start(bf16[512,256]{1,0:T(8,128)(2,1)} %collective-permute-done.12.refs_2_.refs_1_), channel_id=1, source_target_pairs={{28,0},{0,4},{4,8},{8,12},{12,16},{16,20},{20,24},{24,28},{29,1},{... | collective-permute-start | bytes 786440 | tf_op jit(solution)/shard_map/ppermute | solution.py:259
  57.1 9.2 %collective-permute-start.11 = (bf16[512,256]{1,0:T(8,128)(2,1)}, bf16[512,256]{1,0:T(8,128)(2,1)S(1)}, u32[]{:S(2)}, u32[]{:S(2)}) collective-permute-start(bf16[512,256]{1,0:T(8,128)(2,1)} %collective-permute-done.6.refs_1_.refs_0_), channel_id=1, source_target_pairs={{4,0},{8,4},{12,8},{16,12},{20,16},{24,20},{28,24},{0,28},{5,1},{9... | collective-permute-start | bytes 786440 | tf_op jit(solution)/shard_map/ppermute | solution.py:259
  59.8 0.9 copy-start.24
  60.7 1.1 copy-start.27
  61.9 7.3 %copy-start.8 = (bf16[128,1024]{1,0:T(8,128)(2,1)S(1)}, bf16[128,1024]{1,0:T(8,128)(2,1)}, u32[]{:S(2)}) copy-start(bf16[128,1024]{1,0:T(8,128)(2,1)} %copy-done.7) | copy-start | bytes 786436
  61.9 7.3 %copy-start.10 = (bf16[128,1024]{1,0:T(8,128)(2,1)S(1)}, bf16[128,1024]{1,0:T(8,128)(2,1)}, u32[]{:S(2)}) copy-start(bf16[128,1024]{1,0:T(8,128)(2,1)} %copy-done.9) | copy-start | bytes 786436
  61.9 7.3 %copy-start.12 = (bf16[128,1024]{1,0:T(8,128)(2,1)S(1)}, bf16[128,1024]{1,0:T(8,128)(2,1)}, u32[]{:S(2)}) copy-start(bf16[128,1024]{1,0:T(8,128)(2,1)} %copy-done.11) | copy-start | bytes 786436
  61.9 7.3 %copy-start.16 = (bf16[64,1024]{1,0:T(8,128)(2,1)S(1)}, bf16[64,1024]{1,0:T(8,128)(2,1)}, u32[]{:S(2)}) copy-start(bf16[64,1024]{1,0:T(8,128)(2,1)} %copy-done.15) | copy-start | bytes 393220
  61.9 7.3 %copy-start.18 = (bf16[64,1024]{1,0:T(8,128)(2,1)S(1)}, bf16[64,1024]{1,0:T(8,128)(2,1)}, u32[]{:S(2)}) copy-start(bf16[64,1024]{1,0:T(8,128)(2,1)} %copy-done.17) | copy-start | bytes 393220
  66.1 5.5 %collective-permute-start.15 = (bf16[256,256]{1,0:T(8,128)(2,1)S(1)}, bf16[256,256]{1,0:T(8,128)(2,1)S(1)}, u32[]{:S(2)}, u32[]{:S(2)}) collective-permute-start(bf16[256,256]{1,0:T(8,128)(2,1)S(1)} %slice.96), channel_id=1, source_target_pairs={{28,0},{0,4},{4,8},{8,12},{12,16},{16,20},{20,24},{24,28},{29,1},{... | collective-permute-start | bytes 393224 | tf_op jit(solution)/shard_map/ppermute | solution.py:259
  66.4 3.3 %copy-start.21 = (s32[2]{0:T(128)S(1)}, s32[2]{0:T(128)}, u32[]{:S(2)}) copy-start(s32[2]{0:T(128)} %constant.74.clone.number_ref) | copy-start | bytes 28
  66.4 3.3 %copy-start.25 = (bf16[512,128]{1,0:T(8,128)(2,1)S(1)}, bf16[512,128]{1,0:T(8,128)(2,1)}, u32[]{:S(2)}) copy-start(bf16[512,128]{1,0:T(8,128)(2,1)} %copy-done.23) | copy-start | bytes 393220
  66.4 5.1 %collective-permute-start.13 = (bf16[256,256]{1,0:T(8,128)(2,1)S(1)}, bf16[256,256]{1,0:T(8,128)(2,1)S(1)}, u32[]{:S(2)}, u32[]{:S(2)}) collective-permute-start(bf16[256,256]{1,0:T(8,128)(2,1)S(1)} %slice.95), channel_id=1, source_target_pairs={{4,0},{8,4},{12,8},{16,12},{20,16},{24,20},{28,24},{0,28},{5,1},{9... | collective-permute-start | bytes 393224 | tf_op jit(solution)/shard_map/ppermute | solution.py:259
  72.9 13.4 %collective-permute-start.23 = (bf16[512,128]{1,0:T(8,128)(2,1)S(1)}, bf16[512,128]{1,0:T(8,128)(2,1)S(1)}, u32[]{:S(2)}, u32[]{:S(2)}) collective-permute-start(bf16[512,128]{1,0:T(8,128)(2,1)S(1)} %get-tuple-element.59.a_ref.refs_0_), channel_id=1, source_target_pairs={{0,2},{1,3},{2,0},{3,1},{4,6},{5,7},{6,4},{7,5},{8,10},{9,11},{10,... | collective-permute-start | bytes 393224 | tf_op jit(solution)/shard_map/ppermute | solution.py:263
  73.0 17.6 %collective-permute-start.22 = (bf16[512,128]{1,0:T(8,128)(2,1)S(1)}, bf16[512,128]{1,0:T(8,128)(2,1)S(1)}, u32[]{:S(2)}, u32[]{:S(2)}) collective-permute-start(bf16[512,128]{1,0:T(8,128)(2,1)S(1)} %get-tuple-element.59.a_ref.refs_0_), channel_id=1, source_target_pairs={{0,1},{1,0},{2,3},{3,2},{4,5},{5,4},{6,7},{7,6},{8,9},{9,8},{10,11... | collective-permute-start | bytes 393224 | tf_op jit(solution)/shard_map/ppermute | solution.py:263
  76.4 7.0 %collective-permute-start.18 = (bf16[256,256]{1,0:T(8,128)(2,1)S(1)}, bf16[256,256]{1,0:T(8,128)(2,1)S(1)}, u32[]{:S(2)}, u32[]{:S(2)}) collective-permute-start(bf16[256,256]{1,0:T(8,128)(2,1)S(1)} %get-tuple-element.91), channel_id=1, source_target_pairs={{28,0},{0,4},{4,8},{8,12},{12,16},{16,20},{20,24},{24,28},{29,1},{... | collective-permute-start | bytes 393224 | tf_op jit(solution)/shard_map/ppermute | solution.py:259
  76.5 6.9 %collective-permute-start.20 = (bf16[256,256]{1,0:T(8,128)(2,1)S(1)}, bf16[256,256]{1,0:T(8,128)(2,1)S(1)}, u32[]{:S(2)}, u32[]{:S(2)}) collective-permute-start(bf16[256,256]{1,0:T(8,128)(2,1)S(1)} %get-tuple-element.90), channel_id=1, source_target_pairs={{4,0},{8,4},{12,8},{16,12},{20,16},{24,20},{28,24},{0,28},{5,1},{9... | collective-permute-start | bytes 393224 | tf_op jit(solution)/shard_map/ppermute | solution.py:259
  82.2 16.9 %collective-permute-start.16 = (bf16[2,128,1024]{2,1,0:T(8,128)(2,1)S(1)}, bf16[2,128,1024]{2,1,0:T(8,128)(2,1)S(1)}, u32[]{:S(2)}, u32[]{:S(2)}) collective-permute-start(bf16[2,128,1024]{2,1,0:T(8,128)(2,1)S(1)} %get-tuple-element.62), channel_id=1, source_target_pairs={{0,1},{1,0},{2,3},{3,2},{4,5},{5,4},{6,7},{7,6},{8,9},{9,8},{10,11... | collective-permute-start | bytes 1572872 | tf_op jit(solution)/shard_map/ppermute | solution.py:263
  83.4 8.9 %collective-permute-start.19 = (bf16[512,256]{1,0:T(8,128)(2,1)S(1)}, bf16[512,256]{1,0:T(8,128)(2,1)S(1)}, u32[]{:S(2)}, u32[]{:S(2)}) collective-permute-start(bf16[512,256]{1,0:T(8,128)(2,1)S(1)} %pad_maximum_fusion.2), channel_id=1, source_target_pairs={{28,0},{0,4},{4,8},{8,12},{12,16},{16,20},{20,24},{24,28},{29,1},{... | collective-permute-start | bytes 786440 | tf_op jit(solution)/shard_map/ppermute | solution.py:259
  85.8 6.8 %collective-permute-start.21 = (bf16[512,256]{1,0:T(8,128)(2,1)S(1)}, bf16[512,256]{1,0:T(8,128)(2,1)S(1)}, u32[]{:S(2)}, u32[]{:S(2)}) collective-permute-start(bf16[512,256]{1,0:T(8,128)(2,1)S(1)} %pad_maximum_fusion.3), channel_id=1, source_target_pairs={{4,0},{8,4},{12,8},{16,12},{20,16},{24,20},{28,24},{0,28},{5,1},{9... | collective-permute-start | bytes 786440 | tf_op jit(solution)/shard_map/ppermute | solution.py:259
  86.3 4.3 %collective-permute-start.24 = (bf16[512,128]{1,0:T(8,128)(2,1)S(1)}, bf16[512,128]{1,0:T(8,128)(2,1)S(1)}, u32[]{:S(2)}, u32[]{:S(2)}) collective-permute-start(bf16[512,128]{1,0:T(8,128)(2,1)S(1)} %collective-permute-done.23.refs_2_), channel_id=1, source_target_pairs={{0,1},{1,0},{2,3},{3,2},{4,5},{5,4},{6,7},{7,6},{8,9},{9,8},{10,11... | collective-permute-start | bytes 393224 | tf_op jit(solution)/shard_map/ppermute | solution.py:263
  92.3 3.2 %copy-start.4 = (bf16[512,256]{1,0:T(8,128)(2,1)S(1)}, bf16[512,256]{1,0:T(8,128)(2,1)}, u32[]{:S(2)}) copy-start(bf16[512,256]{1,0:T(8,128)(2,1)} %copy-done.3) | copy-start | bytes 786436
  92.4 3.2 %copy-start.6 = (bf16[512,256]{1,0:T(8,128)(2,1)S(1)}, bf16[512,256]{1,0:T(8,128)(2,1)}, u32[]{:S(2)}) copy-start(bf16[512,256]{1,0:T(8,128)(2,1)} %copy-done.5) | copy-start | bytes 786436
  92.4 3.2 %copy-start.19 = (s32[3]{0:T(128)S(1)}, s32[3]{0:T(128)}, u32[]{:S(2)}) copy-start(s32[3]{0:T(128)} %constant.76.clone.number_ref) | copy-start | bytes 40
  92.8 8.0 %collective-permute-start.25 = (bf16[512,256]{1,0:T(8,128)(2,1)S(1)}, bf16[512,256]{1,0:T(8,128)(2,1)S(1)}, u32[]{:S(2)}, u32[]{:S(2)}) collective-permute-start(bf16[512,256]{1,0:T(8,128)(2,1)S(1)} %get-tuple-element.85), channel_id=1, source_target_pairs={{28,0},{0,4},{4,8},{8,12},{12,16},{16,20},{20,24},{24,28},{29,1},{... | collective-permute-start | bytes 786440 | tf_op jit(solution)/shard_map/ppermute | solution.py:259
  94.0 6.8 %collective-permute-start.27 = (bf16[512,256]{1,0:T(8,128)(2,1)S(1)}, bf16[512,256]{1,0:T(8,128)(2,1)S(1)}, u32[]{:S(2)}, u32[]{:S(2)}) collective-permute-start(bf16[512,256]{1,0:T(8,128)(2,1)S(1)} %get-tuple-element.84), channel_id=1, source_target_pairs={{4,0},{8,4},{12,8},{16,12},{20,16},{24,20},{28,24},{0,28},{5,1},{9... | collective-permute-start | bytes 786440 | tf_op jit(solution)/shard_map/ppermute | solution.py:259
  99.3 5.3 %collective-permute-start.17 = (bf16[128,1024]{1,0:T(8,128)(2,1)S(1)}, bf16[128,1024]{1,0:T(8,128)(2,1)S(1)}, u32[]{:S(2)}, u32[]{:S(2)}) collective-permute-start(bf16[128,1024]{1,0:T(8,128)(2,1)S(1)} %get-tuple-element.64), channel_id=1, source_target_pairs={{0,2},{1,3},{2,0},{3,1},{4,6},{5,7},{6,4},{7,5},{8,10},{9,11},{10,... | collective-permute-start | bytes 786440 | tf_op jit(solution)/shard_map/ppermute | solution.py:263
  100.9 6.5 %collective-permute-start.26 = (bf16[512,256]{1,0:T(8,128)(2,1)S(1)}, bf16[512,256]{1,0:T(8,128)(2,1)S(1)}, u32[]{:S(2)}, u32[]{:S(2)}) collective-permute-start(bf16[512,256]{1,0:T(8,128)(2,1)S(1)} %get-tuple-element.82), channel_id=1, source_target_pairs={{28,0},{0,4},{4,8},{8,12},{12,16},{16,20},{20,24},{24,28},{29,1},{... | collective-permute-start | bytes 786440 | tf_op jit(solution)/shard_map/ppermute | solution.py:259
  101.5 5.9 %collective-permute-start.28 = (bf16[512,256]{1,0:T(8,128)(2,1)S(1)}, bf16[512,256]{1,0:T(8,128)(2,1)S(1)}, u32[]{:S(2)}, u32[]{:S(2)}) collective-permute-start(bf16[512,256]{1,0:T(8,128)(2,1)S(1)} %get-tuple-element.83), channel_id=1, source_target_pairs={{4,0},{8,4},{12,8},{16,12},{20,16},{24,20},{28,24},{0,28},{5,1},{9... | collective-permute-start | bytes 786440 | tf_op jit(solution)/shard_map/ppermute | solution.py:259
  109.1 15.4 %all-to-all-start.1 = ((bf16[8,128,512]{2,1,0:T(8,128)(2,1)}), bf16[8,128,512]{2,1,0:T(8,128)(2,1)}, u32[]{:S(2)}, u32[]{:S(2)}) async-start(bf16[8,128,512]{2,1,0:T(8,128)(2,1)} %pad_maximum_fusion), calls=%async_computation.1 | async-start | bytes 2097152 | tf_op jit(solution)/shard_map/all_to_all | solution.py:304
  114.2 5.6 %collective-permute-start.29 = (bf16[2,128,1024]{2,1,0:T(8,128)(2,1)S(1)}, bf16[2,128,1024]{2,1,0:T(8,128)(2,1)S(1)}, u32[]{:S(2)}, u32[]{:S(2)}) collective-permute-start(bf16[2,128,1024]{2,1,0:T(8,128)(2,1)S(1)} %get-tuple-element.77), channel_id=1, source_target_pairs={{0,1},{1,0},{2,3},{3,2},{4,5},{5,4},{6,7},{7,6},{8,9},{9,8},{10,11... | collective-permute-start | bytes 1572872 | tf_op jit(solution)/shard_map/ppermute | solution.py:263
  127.3 14.1 %collective-permute-start.30 = (bf16[128,1024]{1,0:T(8,128)(2,1)S(1)}, bf16[128,1024]{1,0:T(8,128)(2,1)S(1)}, u32[]{:S(2)}, u32[]{:S(2)}) collective-permute-start(bf16[128,1024]{1,0:T(8,128)(2,1)S(1)} %get-tuple-element.80), channel_id=1, source_target_pairs={{0,2},{1,3},{2,0},{3,1},{4,6},{5,7},{6,4},{7,5},{8,10},{9,11},{10,... | collective-permute-start | bytes 786440 | tf_op jit(solution)/shard_map/ppermute | solution.py:263
  129.1 21.6 %all-to-all-start.2 = ((bf16[32,4,512]{2,1,0:T(4,128)(2,1)}), bf16[32,4,512]{2,1,0:T(4,128)(2,1)S(1)}, u32[]{:S(2)}, u32[]{:S(2)}) async-start(bf16[32,4,512]{2,1,0:T(4,128)(2,1)} %copy_dynamic-update-slice_fusion), calls=%async_computation.2 | async-start | bytes 262144 | tf_op jit(solution)/shard_map/all_to_all | solution.py:304
  (1 other events, 0.6 us)
where the time goes:
time: 153 us; the launch traced here: 152 us
  starting transfers between devices  76.3 us (50%)
  waiting for transfers between devices  32.4 us (21%)
  Pallas kernels  22.1 us (14%)
  local copies, waits for them, and re-layouts  13.9 us (9%)
  other arithmetic  4.71 us (3%)
    ppermute x16, starting transfers between devices, take(): return lax.ppermute(x, axis, [((i + by) % size, i) for i in range(size)])  25.7 us
    all_to_all x3, starting transfers between devices, exchange(): return lax.all_to_all(x, axis, split_axis=0, concat_axis=0, tiled=True)  22.8 us
    pallas_call x15, Pallas kernels, call(): pl.pallas_call(kernel, name=name, out_shape=out_shape, in_specs=specs, ou...  22.1 us
    ppermute x13, starting transfers between devices, swap(): return lax.ppermute(x, 'h', [(i, i ^ bit) for i in range(HEADS)])  20.9 us
    all_to_all x3, waiting for transfers between devices, exchange(): return lax.all_to_all(x, axis, split_axis=0, concat_axis=0, tiled=True)  13.1 us
    ppermute x16, waiting for transfers between devices, take(): return lax.ppermute(x, axis, [((i + by) % size, i) for i in range(size)])  10.5 us
    unnamed x63, local copies, waits for them, and re-layouts  8.73 us
    ppermute x2, starting transfers between devices, half_of_head(): return lax.ppermute(after(w_out, x_near[2]), ('f', 'h'), pairs)  6.83 us
  transfers between devices with their start and end apart: 34, of which 11 were waited for; matrix products, arithmetic and copies ran while one was open for 4% of the time, Pallas kernels for 13%

commit v1 on v0

--- a/solution.py
+++ b/solution.py
@@ -176,14 +176,16 @@
     return [copy.wait for copy in copies]
 
 
-def tokens_kernel(*refs):
-    blocks, (w_ref, kv_ref, q_ref, x_ref) = refs[:HEADS], refs[HEADS:]
+def rows_kernel(*refs):
+    blocks, (x_ref,) = refs[:HEADS], refs[HEADS:]
     for d, block in enumerate(blocks):
-        rows = pl.ds(d * block.shape[0], block.shape[0])
-        x_ref[rows, :] = block[...]
-        kvq = dot(block[...], w_ref[...]).astype(BF)
-        kv_ref[rows, :] = kvq[:, : 2 * HD]
-        q_ref[rows, :] = kvq[:, 2 * HD :]
+        x_ref[pl.ds(d * block.shape[0], block.shape[0]), :] = block[...]
+
+
+def tokens_kernel(x_ref, w_ref, kv_ref, q_ref):
+    kvq = dot(x_ref[...], w_ref[...]).astype(BF)
+    kv_ref[...] = kvq[:, : 2 * HD]
+    q_ref[...] = kvq[:, 2 * HD :]
 
 
 def cotangent_kernel(f_ref, a_ref, b_ref, *refs):
@@ -221,6 +223,14 @@
                 ]
 
 
+def clips_kernel(got_ref, out_ref):
+    total = functools.reduce(jnp.add, [got_ref[f].astype(F32) for f in range(NF)])
+    out_ref[:, :, : 3 * HD] = total[:, : 3 * HD].reshape(32, 4, 3 * HD).astype(BF)
+    rows_o = total[:, 3 * HD :].reshape(64, 2, HD).astype(BF)
+    out_ref[:, 0:2, 3 * HD :] = rows_o[:32]
+    out_ref[:, 2:4, 3 * HD :] = rows_o[32:]
+
+
 def heads_kernel(transposed, a_ref, w_ref, own_ref, send_ref):
     terms = (dot_nt if transposed else dot)(a_ref[...], w_ref[...])
     size = ROWS // HEADS
@@ -377,29 +387,18 @@
     halves = half_of_head(0), half_of_head(1)
     mine = jnp.concatenate([head(w_key), head(w_value), head(w_query)], axis=1)
     w_head = spread(mine, "f", NF).reshape(1024, 3 * HD)
-    kv, q, x = call(
+    x = call(rows_kernel, "rows", model_rows, [], work // 4, *x_near)
+    kv, q = call(
         tokens_kernel,
         "tokens",
-        (pair_rows, head_rows, model_rows),
+        (pair_rows, head_rows),
         [],
         3 * work,
-        *x_near,
-        after(w_head, bias_q, bias_b, *halves),
+        x,
+        after(w_head, x, bias_q, bias_b, *halves),
     )
     kv_ring = Ring(kv)
     kv_ring.step()
-    dy_near = gather(after(dy_own, kv))
-    g, dy, out_head = call(
-        cotangent_kernel,
-        "cotangent",
-        (head_rows, model_rows, jax.ShapeDtypeStruct((HD, 1024), BF)),
-        [],
-        2 * work,
-        lax.axis_index("f").reshape(1),
-        *halves,
-        *dy_near,
-    )
-
     def forward(number, state, *more, q=q):
         at_once = 1
         pieces = kv_ring.pieces(number)
@@ -426,12 +425,22 @@
             there=range(2, 2 + len(pieces)),
         )
 
+    dy_near = gather(after(dy_own, *kv_ring.blocks[1], *kv_ring.blocks[7]))
+    g, dy, out_head = call(
+        cotangent_kernel,
+        "cotangent",
+        (head_rows, model_rows, jax.ShapeDtypeStruct((HD, 1024), BF)),
+        [],
+        2 * work,
+        lax.axis_index("f").reshape(1),
+        *halves,
+        *dy_near,
+    )
     kv_ring.step()
-    state = (forward((0, 1, 7), (), q=after(q, *dy_near)),)
+    state = (forward((0, 1, 7), ()),)
     kv_ring.step(*state)
-    state = (forward((2, 6), state),)
-    kv_ring.step(*state)
-    state = (forward((3, 5), state),)
+    kv_ring.step()
+    state = (forward((2, 6, 3, 5), state),)
     att, stat = forward((4,), state, g)
 
     def backward(number, acc, last=False):
@@ -465,6 +474,7 @@
     up = take(part[0, :half], "z", NZ, -1)
     down = take(part[0, half:], "z", NZ, 1)
     part, acc = backward((3, 5), (acc,))
+    sent = acc
     up = jnp.concatenate([add(part[0, :half], up), part[0, half:]], axis=0)
     down = jnp.concatenate([part[1, :half], add(part[1, half:], down)], axis=0)
     up, down = take(up, "z", NZ, -1), take(down, "z", NZ, 1)
@@ -489,7 +499,7 @@
         ],
         2 * work,
         h.reshape(1),
-        *gather(att),
+        *gather(after(att, sent)),
         dy,
         there=range(1, HEADS + 2),
     )
@@ -500,12 +510,17 @@
 
     grad_kv = dot_tn(x, dkv).astype(BF).reshape(NF, HD, 2 * HD)
     terms = jnp.concatenate([grad_q, grad_kv, grad_o], axis=2)
-    got = jnp.sum(exchange(terms, "f").astype(F32), axis=0).astype(BF)
-    got_o = jnp.transpose(got[:, 3 * HD :].reshape(2, 32, 2, HD), (1, 0, 2, 3)).reshape(32, 4, HD)
-    got = jnp.concatenate([got[:, : 3 * HD].reshape(32, 4, 3 * HD), got_o], axis=2)
+    got = call(
+        clips_kernel,
+        "clips_sum",
+        jax.ShapeDtypeStruct((32, 4, 4 * HD), BF),
+        [],
+        10**8,
+        exchange(terms, "f"),
+    )
     d_head = jnp.concatenate([after(dkv, terms), dq], axis=1)
     token_grad = heads_terms(d_head, w_head, True)
-    token_grad = (dy_own.astype(F32) + add_heads(*token_grad, got)).astype(BF)
+    token_grad = (dy_own.astype(F32) + add_heads(*token_grad)).astype(BF)
 
     sums = after(exchange(got, ("z", "h")), token_grad).reshape(NZ, HEADS, 4, 4 * HD)
     sums = jnp.sum(sums.astype(F32), axis=0)

time: 153 us -> 152 us (level)
  waiting for transfers between devices: 32.4 us -> 41.3 us
  local copies, waits for them, and re-layouts: 13.9 us -> 5.54 us
    unnamed x63 -> x48, local copies, waits for them, and re-layouts: 8.73 us -> 1.05 us
    ppermute x16, waiting for transfers between devices: 10.5 us -> 16.8 us  [take(): return lax.ppermute(x, axis, [((i + by) % size, i) for i in range(size)])]
    all_to_all x3, waiting for transfers between devices: 13.1 us -> 15.1 us  [exchange(): return lax.all_to_all(x, axis, split_axis=0, concat_axis=0, tiled=True)]
    pallas_call x15 -> x16, Pallas kernels: 22.1 us -> 23.5 us  [call(): pl.pallas_call(kernel, name=name, out_shape=out_shape, in_specs=specs, ou...]
  transfers between devices with their start and end apart: 34 -> 34, of which waited for: 11 -> 10; matrix products, arithmetic and copies ran while one was open for 4% -> 4% of each run, Pallas kernels for 13% -> 12%
where the time goes in v1:
time: 152 us; the launch traced here: 151 us
  starting transfers between devices  75 us (49%)
  waiting for transfers between devices  41.3 us (27%)
  Pallas kernels  23.5 us (15%)
  local copies, waits for them, and re-layouts  5.54 us (4%)
  other arithmetic  3.4 us (2%)
    ppermute x16, starting transfers between devices, take(): return lax.ppermute(x, axis, [((i + by) % size, i) for i in range(size)])  25.7 us
    pallas_call x16, Pallas kernels, call(): pl.pallas_call(kernel, name=name, out_shape=out_shape, in_specs=specs, ou...  23.5 us
    all_to_all x3, starting transfers between devices, exchange(): return lax.all_to_all(x, axis, split_axis=0, concat_axis=0, tiled=True)  22.2 us
    ppermute x13, starting transfers between devices, swap(): return lax.ppermute(x, 'h', [(i, i ^ bit) for i in range(HEADS)])  20.2 us
    ppermute x16, waiting for transfers between devices, take(): return lax.ppermute(x, axis, [((i + by) % size, i) for i in range(size)])  16.8 us
    all_to_all x3, waiting for transfers between devices, exchange(): return lax.all_to_all(x, axis, split_axis=0, concat_axis=0, tiled=True)  15.1 us
    ppermute x2, starting transfers between devices, half_of_head(): return lax.ppermute(after(w_out, x_near[2]), ('f', 'h'), pairs)  6.84 us
    ppermute x2, waiting for transfers between devices, half_of_head(): return lax.ppermute(after(w_out, x_near[2]), ('f', 'h'), pairs)  6.24 us
  transfers between devices with their start and end apart: 34, of which 10 were waited for; matrix products, arithmetic and copies ran while one was open for 4% of the time, Pallas kernels for 12%

profile of v1, /device:TPU:1, one launch (start us, length us, event | category | flops | bytes accessed | tf_op | source)
XLA Modules:
  0.0 151.4 jit_solution(6535934742009735665)
XLA Ops:
  0.6 2.1 %collective-permute-start.1 = (bf16[128,1024]{1,0:T(8,128)(2,1)}, bf16[128,1024]{1,0:T(8,128)(2,1)S(1)}, u32[]{:S(2)}, u32[]{:S(2)}) collective-permute-start(bf16[128,1024]{1,0:T(8,128)(2,1)} %bitcast.69), channel_id=1, source_target_pairs={{0,2},{1,3},{2,0},{3,1},{4,6},{5,7},{6,4},{7,5},{8,10},{9,11},{10,... | collective-permute-start | bytes 786440 | tf_op jit(solution)/shard_map/ppermute | solution.py:273
  2.8 1.3 collective-permute-start
  4.1 0.8 constant_dynamic-slice_fusion.1
  4.9 1.0 broadcast_in_dim.33
  5.9 6.1 %all-to-all-start = ((bf16[8,128,384]{2,1,0:T(8,128)(2,1)}), bf16[8,128,384]{2,1,0:T(8,128)(2,1)S(1)}, u32[]{:S(2)}, u32[]{:S(2)}) async-start(bf16[8,128,384]{2,1,0:T(8,128)(2,1)} %broadcast_in_dim.33), calls=%async_computation | async-start | bytes 1572864 | tf_op jit(solution)/shard_map/all_to_all | solution.py:314
  12.6 0.1 reshape.106
  12.8 0.4 collective-permute-start.2
  13.2 0.3 fusion
  13.4 3.5 %collective-permute-start.3 = (bf16[64,1024]{1,0:T(8,128)(2,1)}, bf16[64,1024]{1,0:T(8,128)(2,1)S(1)}, u32[]{:S(2)}, u32[]{:S(2)}) collective-permute-start(bf16[64,1024]{1,0:T(8,128)(2,1)} %param.20), channel_id=1, source_target_pairs={{0,0},{64,1},{128,2},{192,3},{1,32},{65,33},{129,34},{193,35},{2,6... | collective-permute-start | bytes 393224 | tf_op jit(solution)/shard_map/ppermute | solution.py:385
  17.0 3.3 %collective-permute-start.4 = (bf16[64,1024]{1,0:T(8,128)(2,1)}, bf16[64,1024]{1,0:T(8,128)(2,1)S(1)}, u32[]{:S(2)}, u32[]{:S(2)}) collective-permute-start(bf16[64,1024]{1,0:T(8,128)(2,1)} %param.20), channel_id=1, source_target_pairs={{32,0},{96,1},{160,2},{224,3},{33,32},{97,33},{161,34},{225,35},{3... | collective-permute-start | bytes 393224 | tf_op jit(solution)/shard_map/ppermute | solution.py:385
  20.5 0.2 broadcast_in_dim.37.refs_4_.refs_5_.refs_3_
  20.9 0.2 broadcast_in_dim.39.refs_2_.refs_3_
  21.2 6.2 %collective-permute-done.3.a_ref = bf16[64,1024]{1,0:T(8,128)(2,1)S(1)} collective-permute-done((bf16[64,1024]{1,0:T(8,128)(2,1)}, bf16[64,1024]{1,0:T(8,128)(2,1)S(1)}, u32[]{:S(2)}, u32[]{:S(2)}) %collective-permute-start.3) | collective-permute-done | bytes 131104 | tf_op jit(solution)/shard_map/ppermute | solution.py:385
  27.5 0.7 tokens.1
  28.3 1.7 %collective-permute-start.7 = (bf16[512,256]{1,0:T(8,128)(2,1)S(1)}, bf16[512,256]{1,0:T(8,128)(2,1)S(1)}, u32[]{:S(2)}, u32[]{:S(2)}) collective-permute-start(bf16[512,256]{1,0:T(8,128)(2,1)S(1)} %get-tuple-element.42.refs_1_.refs_2_), channel_id=1, source_target_pairs={{28,0},{0,4},{4,8},{8,12},{12,16},{16,20},{20,24},{24,28},{29,1},{... | collective-permute-start | bytes 786440 | tf_op jit(solution)/shard_map/ppermute | solution.py:269
  30.0 4.0 %collective-permute-start.5 = (bf16[512,256]{1,0:T(8,128)(2,1)S(1)}, bf16[512,256]{1,0:T(8,128)(2,1)S(1)}, u32[]{:S(2)}, u32[]{:S(2)}) collective-permute-start(bf16[512,256]{1,0:T(8,128)(2,1)S(1)} %get-tuple-element.42.refs_1_.refs_2_), channel_id=1, source_target_pairs={{4,0},{8,4},{12,8},{16,12},{20,16},{24,20},{28,24},{0,28},{5,1},{9... | collective-permute-start | bytes 786440 | tf_op jit(solution)/shard_map/ppermute | solution.py:269
  34.0 6.2 %collective-permute-done.7.refs_3_.refs_1_ = bf16[512,256]{1,0:T(8,128)(2,1)S(1)} collective-permute-done((bf16[512,256]{1,0:T(8,128)(2,1)S(1)}, bf16[512,256]{1,0:T(8,128)(2,1)S(1)}, u32[]{:S(2)}, u32[]{:S(2)}) %collective-permute-start.7) | collective-permute-done | bytes 262176 | tf_op jit(solution)/shard_map/ppermute | solution.py:269
  40.2 3.3 %collective-permute-start.6 = (bf16[512,256]{1,0:T(8,128)(2,1)S(1)}, bf16[512,256]{1,0:T(8,128)(2,1)}, u32[]{:S(2)}, u32[]{:S(2)}) collective-permute-start(bf16[512,256]{1,0:T(8,128)(2,1)S(1)} %collective-permute-done.5.refs_2_.refs_0_), channel_id=1, source_target_pairs={{4,0},{8,4},{12,8},{16,12},{20,16},{24,20},{28,24},{0,28},{5,1},{9... | collective-permute-start | bytes 786440 | tf_op jit(solution)/shard_map/ppermute | solution.py:269
  43.4 4.6 %collective-permute-start.14 = (bf16[128,1024]{1,0:T(8,128)(2,1)S(1)}, bf16[128,1024]{1,0:T(8,128)(2,1)}, u32[]{:S(2)}, u32[]{:S(2)}) collective-permute-start(bf16[128,1024]{1,0:T(8,128)(2,1)S(1)} %bitcast.74), channel_id=1, source_target_pairs={{0,2},{1,3},{2,0},{3,1},{4,6},{5,7},{6,4},{7,5},{8,10},{9,11},{10,... | collective-permute-start | bytes 786440 | tf_op jit(solution)/shard_map/ppermute | solution.py:273
  48.0 2.5 %attn_forward.2.refs_6_ = f32[3,512,128]{2,1,0:T(8,128)S(1)} custom-call(s32[3]{0:T(128)S(1)} %copy-done.17, bf16[512,128]{1,0:T(8,128)(2,1)S(1)} %get-tuple-element.41.refs_0_.q_ref, bf16[512,256]{1,0:T(8,128)(2,1)S(1)} %get-tuple-element.42.refs_1_.refs_2_, bf16[512,256]{1,0:T(8,128)(2,1)S(1)} %collective-permute-done.5.refs_2_.refs_0_, ...), custom_call_target="tpu_custom_call" | custom-call | flops 1610612736 | bytes 1048576 | tf_op jit(solution)/shard_map/attn_forward/pallas_call | solution.py:254
  50.6 0.9 copy-done.20
  51.5 2.7 %collective-permute-start.8 = (bf16[512,256]{1,0:T(8,128)(2,1)}, bf16[512,256]{1,0:T(8,128)(2,1)S(1)}, u32[]{:S(2)}, u32[]{:S(2)}) collective-permute-start(bf16[512,256]{1,0:T(8,128)(2,1)} %collective-permute-done.6.refs_1_.refs_0_), channel_id=1, source_target_pairs={{4,0},{8,4},{12,8},{16,12},{20,16},{24,20},{28,24},{0,28},{5,1},{9... | collective-permute-start | bytes 786440 | tf_op jit(solution)/shard_map/ppermute | solution.py:269
  54.2 1.4 collective-permute-start.13
  55.6 4.4 %collective-permute-done.11.refs_4_.refs_1_ = bf16[512,256]{1,0:T(8,128)(2,1)S(1)} collective-permute-done((bf16[512,256]{1,0:T(8,128)(2,1)}, bf16[512,256]{1,0:T(8,128)(2,1)S(1)}, u32[]{:S(2)}, u32[]{:S(2)}) %collective-permute-start.11) | collective-permute-done | bytes 262176 | tf_op jit(solution)/shard_map/ppermute | solution.py:269
  60.1 2.9 %collective-permute-start.9 = (bf16[256,256]{1,0:T(8,128)(2,1)S(1)}, bf16[256,256]{1,0:T(8,128)(2,1)S(1)}, u32[]{:S(2)}, u32[]{:S(2)}) collective-permute-start(bf16[256,256]{1,0:T(8,128)(2,1)S(1)} %slice.87), channel_id=1, source_target_pairs={{4,0},{8,4},{12,8},{16,12},{20,16},{24,20},{28,24},{0,28},{5,1},{9... | collective-permute-start | bytes 393224 | tf_op jit(solution)/shard_map/ppermute | solution.py:269
  63.0 1.6 %cotangent.1 = (bf16[512,128]{1,0:T(8,128)(2,1)S(1)}, bf16[512,1024]{1,0:T(8,128)(2,1)S(1)}, bf16[128,1024]{1,0:T(8,128)(2,1)S(1)}) custom-call(s32[1]{0:T(128)} %bitcast.5.f_ref, bf16[64,1024]{1,0:T(8,128)(2,1)S(1)} %copy-done.10, bf16[64,1024]{1,0:T(8,128)(2,1)S(1)} %copy-done.12, bf16[128,1024]{1,0:T(8,128)(2,1)S(1)} %bitcast.76, ...), custom_call_target="tpu_custom_call" | custom-call | flops 536870912 | bytes 1048576 | tf_op jit(solution)/shard_map/cotangent/pallas_call | solution.py:254
  64.7 3.9 %attn_forward.3.refs_4_ = f32[3,512,128]{2,1,0:T(8,128)S(1)} custom-call(s32[4]{0:T(128)S(1)} %copy-done.16, bf16[512,128]{1,0:T(8,128)(2,1)S(1)} %copy-done.19, bf16[512,256]{1,0:T(8,128)(2,1)} %collective-permute-done.6.refs_1_.refs_0_, bf16[512,256]{1,0:T(8,128)(2,1)} %collective-permute-done.10.refs_2_.refs_1_, ...), custom_call_target="tpu_custom_call" | custom-call | flops 2147483648 | bytes 1048576 | tf_op jit(solution)/shard_map/attn_forward/pallas_call | solution.py:254
  68.7 1.3 attn_forward_end.1
  70.0 1.2 attn_backward.4
  71.2 2.2 %attn_backward.5 = (bf16[2,512,256]{2,1,0:T(8,128)(2,1)S(1)}, f32[128,512]{1,0:T(8,128)S(1)}) custom-call(bf16[512,128]{1,0:T(8,128)(2,1)S(1)} %copy-done.19, bf16[512,128]{1,0:T(8,128)(2,1)S(1)} %get-tuple-element.46.refs_5_.g_ref, f32[2,512]{1,0:T(2,128)S(1)} %get-tuple-element.48.stat_ref, s32[2]{0:T(128)S(1)} %copy-done.15, ...), custom_call_target="tpu_custom_call" | custom-call | flops 2684354560 | bytes 1048576 | tf_op jit(solution)/shard_map/attn_backward/pallas_call | solution.py:254
  73.4 3.0 %collective-permute-start.23 = (bf16[512,128]{1,0:T(8,128)(2,1)S(1)}, bf16[512,128]{1,0:T(8,128)(2,1)S(1)}, u32[]{:S(2)}, u32[]{:S(2)}) collective-permute-start(bf16[512,128]{1,0:T(8,128)(2,1)S(1)} %get-tuple-element.51.a_ref.refs_0_), channel_id=1, source_target_pairs={{0,2},{1,3},{2,0},{3,1},{4,6},{5,7},{6,4},{7,5},{8,10},{9,11},{10,... | collective-permute-start | bytes 393224 | tf_op jit(solution)/shard_map/ppermute | solution.py:273
  76.4 2.4 %collective-permute-start.22 = (bf16[512,128]{1,0:T(8,128)(2,1)S(1)}, bf16[512,128]{1,0:T(8,128)(2,1)S(1)}, u32[]{:S(2)}, u32[]{:S(2)}) collective-permute-start(bf16[512,128]{1,0:T(8,128)(2,1)S(1)} %get-tuple-element.51.a_ref.refs_0_), channel_id=1, source_target_pairs={{0,1},{1,0},{2,3},{3,2},{4,5},{5,4},{6,7},{7,6},{8,9},{9,8},{10,11... | collective-permute-start | bytes 393224 | tf_op jit(solution)/shard_map/ppermute | solution.py:273
  78.9 2.7 %collective-permute-start.20 = (bf16[256,256]{1,0:T(8,128)(2,1)S(1)}, bf16[256,256]{1,0:T(8,128)(2,1)S(1)}, u32[]{:S(2)}, u32[]{:S(2)}) collective-permute-start(bf16[256,256]{1,0:T(8,128)(2,1)S(1)} %get-tuple-element.80), channel_id=1, source_target_pairs={{4,0},{8,4},{12,8},{16,12},{20,16},{24,20},{28,24},{0,28},{5,1},{9... | collective-permute-start | bytes 393224 | tf_op jit(solution)/shard_map/ppermute | solution.py:269
  81.6 0.4 heads_terms.2
  82.0 0.7 collective-permute-start.16
  82.7 2.6 %collective-permute-done.18 = bf16[256,256]{1,0:T(8,128)(2,1)S(1)} collective-permute-done((bf16[256,256]{1,0:T(8,128)(2,1)S(1)}, bf16[256,256]{1,0:T(8,128)(2,1)S(1)}, u32[]{:S(2)}, u32[]{:S(2)}) %collective-permute-start.18) | collective-permute-done | bytes 131104 | tf_op jit(solution)/shard_map/ppermute | solution.py:269
  85.5 2.7 %collective-permute-start.21 = (bf16[512,256]{1,0:T(8,128)(2,1)S(1)}, bf16[512,256]{1,0:T(8,128)(2,1)S(1)}, u32[]{:S(2)}, u32[]{:S(2)}) collective-permute-start(bf16[512,256]{1,0:T(8,128)(2,1)S(1)} %pad_maximum_fusion.3), channel_id=1, source_target_pairs={{4,0},{8,4},{12,8},{16,12},{20,16},{24,20},{28,24},{0,28},{5,1},{9... | collective-permute-start | bytes 786440 | tf_op jit(solution)/shard_map/ppermute | solution.py:269
  88.2 1.3 collective-permute-start.24
  89.5 3.1 %attn_backward.6 = (bf16[2,512,256]{2,1,0:T(8,128)(2,1)S(1)}, f32[128,512]{1,0:T(8,128)S(1)}) custom-call(bf16[512,128]{1,0:T(8,128)(2,1)S(1)} %copy-done.19, bf16[512,128]{1,0:T(8,128)(2,1)S(1)} %get-tuple-element.46.refs_5_.g_ref, f32[2,512]{1,0:T(2,128)S(1)} %get-tuple-element.48.stat_ref, s32[2]{0:T(128)S(1)} %copy-done.14, ...), custom_call_target="tpu_custom_call" | custom-call | flops 2684354560 | bytes 1048576 | tf_op jit(solution)/shard_map/attn_backward/pallas_call | solution.py:254
  92.6 1.7 %grad_out.1 = bf16[8,128,128]{2,1,0:T(8,128)(2,1)S(1)} custom-call(s32[1]{0:T(128)} %bitcast.18.h_ref, bf16[512,128]{1,0:T(8,128)(2,1)S(1)} %get-tuple-element.51.a_ref.refs_0_, bf16[512,128]{1,0:T(8,128)(2,1)S(1)} %collective-permute-done.22.refs_1_, bf16[512,128]{1,0:T(8,128)(2,1)S(1)} %collective-permute-done.23.refs_2_, ...), custom_call_target="tpu_custom_call" | custom-call | flops 536870912 | bytes 1048576 | tf_op jit(solution)/shard_map/grad_out/pallas_call | solution.py:254
  94.4 0.1 fusion.5
  94.6 0.8 collective-permute-start.25
  95.4 1.9 %collective-permute-start.27 = (bf16[512,256]{1,0:T(8,128)(2,1)S(1)}, bf16[512,256]{1,0:T(8,128)(2,1)S(1)}, u32[]{:S(2)}, u32[]{:S(2)}) collective-permute-start(bf16[512,256]{1,0:T(8,128)(2,1)S(1)} %get-tuple-element.74), channel_id=1, source_target_pairs={{4,0},{8,4},{12,8},{16,12},{20,16},{24,20},{28,24},{0,28},{5,1},{9... | collective-permute-start | bytes 786440 | tf_op jit(solution)/shard_map/ppermute | solution.py:269
  97.4 3.1 %attn_backward.7 = (bf16[3,512,256]{2,1,0:T(8,128)(2,1)S(1)}, bf16[512,128]{1,0:T(8,128)(2,1)S(1)}) custom-call(bf16[512,128]{1,0:T(8,128)(2,1)S(1)} %copy-done.19, bf16[512,128]{1,0:T(8,128)(2,1)S(1)} %get-tuple-element.46.refs_5_.g_ref, f32[2,512]{1,0:T(2,128)S(1)} %get-tuple-element.48.stat_ref, s32[3]{0:T(128)S(1)} %copy-done.13, ...), custom_call_target="tpu_custom_call" | custom-call | flops 4026531840 | bytes 1048576 | tf_op jit(solution)/shard_map/attn_backward/pallas_call | solution.py:254
  100.5 0.5 convolution_convert_fusion.1
  101.2 1.6 %collective-permute-done.25 = bf16[512,256]{1,0:T(8,128)(2,1)S(1)} collective-permute-done((bf16[512,256]{1,0:T(8,128)(2,1)S(1)}, bf16[512,256]{1,0:T(8,128)(2,1)S(1)}, u32[]{:S(2)}, u32[]{:S(2)}) %collective-permute-start.25) | collective-permute-done | bytes 262176 | tf_op jit(solution)/shard_map/ppermute | solution.py:269
  102.8 0.1 fusion.4
  103.0 2.7 %collective-permute-start.28 = (bf16[512,256]{1,0:T(8,128)(2,1)S(1)}, bf16[512,256]{1,0:T(8,128)(2,1)S(1)}, u32[]{:S(2)}, u32[]{:S(2)}) collective-permute-start(bf16[512,256]{1,0:T(8,128)(2,1)S(1)} %get-tuple-element.73), channel_id=1, source_target_pairs={{4,0},{8,4},{12,8},{16,12},{20,16},{24,20},{28,24},{0,28},{5,1},{9... | collective-permute-start | bytes 786440 | tf_op jit(solution)/shard_map/ppermute | solution.py:269
  105.7 1.6 %collective-permute-done.17 = bf16[128,1024]{1,0:T(8,128)(2,1)S(1)} collective-permute-done((bf16[128,1024]{1,0:T(8,128)(2,1)S(1)}, bf16[128,1024]{1,0:T(8,128)(2,1)S(1)}, u32[]{:S(2)}, u32[]{:S(2)}) %collective-permute-start.17) | collective-permute-done | bytes 262176 | tf_op jit(solution)/shard_map/ppermute | solution.py:273
  107.3 0.8 add_convert_fusion.2
  108.2 2.0 %collective-permute-done.26 = bf16[512,256]{1,0:T(8,128)(2,1)S(1)} collective-permute-done((bf16[512,256]{1,0:T(8,128)(2,1)S(1)}, bf16[512,256]{1,0:T(8,128)(2,1)S(1)}, u32[]{:S(2)}, u32[]{:S(2)}) %collective-permute-start.26) | collective-permute-done | bytes 262176 | tf_op jit(solution)/shard_map/ppermute | solution.py:269
  110.3 0.5 convolution_convert_fusion
  110.8 1.1 pad_maximum_fusion
  111.9 3.6 %all-to-all-start.1 = ((bf16[8,128,512]{2,1,0:T(8,128)(2,1)}), bf16[8,128,512]{2,1,0:T(8,128)(2,1)S(1)}, u32[]{:S(2)}, u32[]{:S(2)}) async-start(bf16[8,128,512]{2,1,0:T(8,128)(2,1)} %pad_maximum_fusion), calls=%async_computation.1 | async-start | bytes 2097152 | tf_op jit(solution)/shard_map/all_to_all | solution.py:314
  115.5 0.7 heads_terms.3
  116.3 2.8 %collective-permute-start.29 = (bf16[2,128,1024]{2,1,0:T(8,128)(2,1)S(1)}, bf16[2,128,1024]{2,1,0:T(8,128)(2,1)S(1)}, u32[]{:S(2)}, u32[]{:S(2)}) collective-permute-start(bf16[2,128,1024]{2,1,0:T(8,128)(2,1)S(1)} %get-tuple-element.68), channel_id=1, source_target_pairs={{0,1},{1,0},{2,3},{3,2},{4,5},{5,4},{6,7},{7,6},{8,9},{9,8},{10,11... | collective-permute-start | bytes 1572872 | tf_op jit(solution)/shard_map/ppermute | solution.py:273
  119.1 1.5 %collective-permute-done.29.got_ref = bf16[2,128,1024]{2,1,0:T(8,128)(2,1)S(1)} collective-permute-done((bf16[2,128,1024]{2,1,0:T(8,128)(2,1)S(1)}, bf16[2,128,1024]{2,1,0:T(8,128)(2,1)S(1)}, u32[]{:S(2)}, u32[]{:S(2)}) %collective-permute-start.29) | collective-permute-done | bytes 524320 | tf_op jit(solution)/shard_map/ppermute | solution.py:273
  120.9 6.7 %all-to-all-done.1.got_ref = bf16[8,128,512]{2,1,0:T(8,128)(2,1)S(1)} async-done(((bf16[8,128,512]{2,1,0:T(8,128)(2,1)}), bf16[8,128,512]{2,1,0:T(8,128)(2,1)S(1)}, u32[]{:S(2)}, u32[]{:S(2)}) %all-to-all-start.1) | async-done | bytes 1048608 | tf_op jit(solution)/shard_map/all_to_all | solution.py:314
  127.5 0.8 clips_sum.1
  128.3 12.5 %all-to-all-start.2 = ((bf16[32,4,512]{2,1,0:T(4,128)(2,1)}), bf16[32,4,512]{2,1,0:T(4,128)(2,1)S(1)}, u32[]{:S(2)}, u32[]{:S(2)}) async-start(bf16[32,4,512]{2,1,0:T(4,128)(2,1)} %clips_sum.1), calls=%async_computation.2 | async-start | bytes 262144 | tf_op jit(solution)/shard_map/all_to_all | solution.py:314
  140.8 0.8 add_convert_fusion
  141.6 8.4 %all-to-all-done.2 = bf16[32,4,512]{2,1,0:T(4,128)(2,1)S(1)} async-done(((bf16[32,4,512]{2,1,0:T(4,128)(2,1)}), bf16[32,4,512]{2,1,0:T(4,128)(2,1)S(1)}, u32[]{:S(2)}, u32[]{:S(2)}) %all-to-all-start.2) | async-done | bytes 131104 | tf_op jit(solution)/shard_map/all_to_all | solution.py:314
  150.2 0.6 slice.93
  150.8 0.6 slice_bitcast_fusion.6
  (112 shorter events, 2.3 us)
Async XLA Ops:
  0.6 3.4 %copy-start = (bf16[128,512]{1,0:T(8,128)(2,1)S(1)}, bf16[128,512]{1,0:T(8,128)(2,1)}, u32[]{:S(2)}) copy-start(bf16[128,512]{1,0:T(8,128)(2,1)} %param.18) | copy-start | bytes 393220
  0.6 12.1 %collective-permute-start.1 = (bf16[128,1024]{1,0:T(8,128)(2,1)}, bf16[128,1024]{1,0:T(8,128)(2,1)S(1)}, u32[]{:S(2)}, u32[]{:S(2)}) collective-permute-start(bf16[128,1024]{1,0:T(8,128)(2,1)} %bitcast.69), channel_id=1, source_target_pairs={{0,2},{1,3},{2,0},{3,1},{4,6},{5,7},{6,4},{7,5},{8,10},{9,11},{10,... | collective-permute-start | bytes 786440 | tf_op jit(solution)/shard_map/ppermute | solution.py:273
  2.8 18.3 %collective-permute-start = (bf16[128,1024]{1,0:T(8,128)(2,1)}, bf16[128,1024]{1,0:T(8,128)(2,1)S(1)}, u32[]{:S(2)}, u32[]{:S(2)}) collective-permute-start(bf16[128,1024]{1,0:T(8,128)(2,1)} %bitcast.70), channel_id=1, source_target_pairs={{0,1},{1,0},{2,3},{3,2},{4,5},{5,4},{6,7},{7,6},{8,9},{9,8},{10,11... | collective-permute-start | bytes 786440 | tf_op jit(solution)/shard_map/ppermute | solution.py:273
  4.9 7.2 %copy-start.22 = (s32[64]{0:T(128)S(1)}, s32[64]{0:T(128)}, u32[]{:S(2)}) copy-start(s32[64]{0:T(128)} %param.22) | copy-start | bytes 772
  5.9 7.2 %copy-start.23 = (s32[32,32]{1,0:T(8,128)S(1)}, s32[32,32]{1,0:T(8,128)}, u32[]{:S(2)}) copy-start(s32[32,32]{1,0:T(8,128)} %param.21) | copy-start | bytes 12292
  5.9 21.6 %all-to-all-start = ((bf16[8,128,384]{2,1,0:T(8,128)(2,1)}), bf16[8,128,384]{2,1,0:T(8,128)(2,1)S(1)}, u32[]{:S(2)}, u32[]{:S(2)}) async-start(bf16[8,128,384]{2,1,0:T(8,128)(2,1)} %broadcast_in_dim.33), calls=%async_computation | async-start | bytes 1572864 | tf_op jit(solution)/shard_map/all_to_all | solution.py:314
  12.1 9.1 %copy-start.1 = (bf16[1,128,1024]{2,1,0:T(8,128)(2,1)S(1)}, bf16[1,128,1024]{2,1,0:T(8,128)(2,1)}, u32[]{:S(2)}) copy-start(bf16[1,128,1024]{2,1,0:T(8,128)(2,1)} %param.15) | copy-start | bytes 786436
  12.8 8.3 %collective-permute-start.2 = (bf16[128,1024]{1,0:T(8,128)(2,1)S(1)}, bf16[128,1024]{1,0:T(8,128)(2,1)S(1)}, u32[]{:S(2)}, u32[]{:S(2)}) collective-permute-start(bf16[128,1024]{1,0:T(8,128)(2,1)S(1)} %collective-permute-done.1.refs_2_), channel_id=1, source_target_pairs={{0,1},{1,0},{2,3},{3,2},{4,5},{5,4},{6,7},{7,6},{8,9},{9,8},{10,11... | collective-permute-start | bytes 786440 | tf_op jit(solution)/shard_map/ppermute | solution.py:273
  13.4 14.0 %collective-permute-start.3 = (bf16[64,1024]{1,0:T(8,128)(2,1)}, bf16[64,1024]{1,0:T(8,128)(2,1)S(1)}, u32[]{:S(2)}, u32[]{:S(2)}) collective-permute-start(bf16[64,1024]{1,0:T(8,128)(2,1)} %param.20), channel_id=1, source_target_pairs={{0,0},{64,1},{128,2},{192,3},{1,32},{65,33},{129,34},{193,35},{2,6... | collective-permute-start | bytes 393224 | tf_op jit(solution)/shard_map/ppermute | solution.py:385
  17.0 10.5 %collective-permute-start.4 = (bf16[64,1024]{1,0:T(8,128)(2,1)}, bf16[64,1024]{1,0:T(8,128)(2,1)S(1)}, u32[]{:S(2)}, u32[]{:S(2)}) collective-permute-start(bf16[64,1024]{1,0:T(8,128)(2,1)} %param.20), channel_id=1, source_target_pairs={{32,0},{96,1},{160,2},{224,3},{33,32},{97,33},{161,34},{225,35},{3... | collective-permute-start | bytes 393224 | tf_op jit(solution)/shard_map/ppermute | solution.py:385
  27.5 0.8 copy-start.9
  27.5 0.8 copy-start.11
  27.5 16.0 %copy-start.2 = (bf16[1,128,1024]{2,1,0:T(8,128)(2,1)S(1)}, bf16[1,128,1024]{2,1,0:T(8,128)(2,1)}, u32[]{:S(2)}) copy-start(bf16[1,128,1024]{2,1,0:T(8,128)(2,1)} %param.16) | copy-start | bytes 786436
  27.5 20.5 %copy-start.17 = (s32[3]{0:T(128)S(1)}, s32[3]{0:T(128)}, u32[]{:S(2)}) copy-start(s32[3]{0:T(128)} %constant.72.clone.number_ref) | copy-start | bytes 40
  28.2 22.3 %copy-start.3 = (bf16[512,256]{1,0:T(8,128)(2,1)}, bf16[512,256]{1,0:T(8,128)(2,1)S(1)}, u32[]{:S(2)}) copy-start(bf16[512,256]{1,0:T(8,128)(2,1)S(1)} %get-tuple-element.42.refs_1_.refs_2_) | copy-start | bytes 786436
  28.2 22.3 %copy-start.18 = (bf16[512,128]{1,0:T(8,128)(2,1)}, bf16[512,128]{1,0:T(8,128)(2,1)S(1)}, u32[]{:S(2)}) copy-start(bf16[512,128]{1,0:T(8,128)(2,1)S(1)} %get-tuple-element.41.refs_0_.q_ref) | copy-start | bytes 393220
  28.3 11.9 %collective-permute-start.7 = (bf16[512,256]{1,0:T(8,128)(2,1)S(1)}, bf16[512,256]{1,0:T(8,128)(2,1)S(1)}, u32[]{:S(2)}, u32[]{:S(2)}) collective-permute-start(bf16[512,256]{1,0:T(8,128)(2,1)S(1)} %get-tuple-element.42.refs_1_.refs_2_), channel_id=1, source_target_pairs={{28,0},{0,4},{4,8},{8,12},{12,16},{16,20},{20,24},{24,28},{29,1},{... | collective-permute-start | bytes 786440 | tf_op jit(solution)/shard_map/ppermute | solution.py:269
  30.0 10.2 %collective-permute-start.5 = (bf16[512,256]{1,0:T(8,128)(2,1)S(1)}, bf16[512,256]{1,0:T(8,128)(2,1)S(1)}, u32[]{:S(2)}, u32[]{:S(2)}) collective-permute-start(bf16[512,256]{1,0:T(8,128)(2,1)S(1)} %get-tuple-element.42.refs_1_.refs_2_), channel_id=1, source_target_pairs={{4,0},{8,4},{12,8},{16,12},{20,16},{24,20},{28,24},{0,28},{5,1},{9... | collective-permute-start | bytes 786440 | tf_op jit(solution)/shard_map/ppermute | solution.py:269
  40.2 10.4 %copy-start.5 = (bf16[512,256]{1,0:T(8,128)(2,1)}, bf16[512,256]{1,0:T(8,128)(2,1)S(1)}, u32[]{:S(2)}) copy-start(bf16[512,256]{1,0:T(8,128)(2,1)S(1)} %collective-permute-done.7.refs_3_.refs_1_) | copy-start | bytes 786436
  40.2 11.3 %collective-permute-start.10 = (bf16[512,256]{1,0:T(8,128)(2,1)S(1)}, bf16[512,256]{1,0:T(8,128)(2,1)}, u32[]{:S(2)}, u32[]{:S(2)}) collective-permute-start(bf16[512,256]{1,0:T(8,128)(2,1)S(1)} %collective-permute-done.7.refs_3_.refs_1_), channel_id=1, source_target_pairs={{28,0},{0,4},{4,8},{8,12},{12,16},{16,20},{20,24},{24,28},{29,1},{... | collective-permute-start | bytes 786440 | tf_op jit(solution)/shard_map/ppermute | solution.py:269
  40.2 10.4 %copy-start.7 = (bf16[512,256]{1,0:T(8,128)(2,1)}, bf16[512,256]{1,0:T(8,128)(2,1)S(1)}, u32[]{:S(2)}) copy-start(bf16[512,256]{1,0:T(8,128)(2,1)S(1)} %collective-permute-done.5.refs_2_.refs_0_) | copy-start | bytes 786436
  40.2 11.3 %collective-permute-start.6 = (bf16[512,256]{1,0:T(8,128)(2,1)S(1)}, bf16[512,256]{1,0:T(8,128)(2,1)}, u32[]{:S(2)}, u32[]{:S(2)}) collective-permute-start(bf16[512,256]{1,0:T(8,128)(2,1)S(1)} %collective-permute-done.5.refs_2_.refs_0_), channel_id=1, source_target_pairs={{4,0},{8,4},{12,8},{16,12},{20,16},{24,20},{28,24},{0,28},{5,1},{9... | collective-permute-start | bytes 786440 | tf_op jit(solution)/shard_map/ppermute | solution.py:269
  43.4 12.1 %collective-permute-start.14 = (bf16[128,1024]{1,0:T(8,128)(2,1)S(1)}, bf16[128,1024]{1,0:T(8,128)(2,1)}, u32[]{:S(2)}, u32[]{:S(2)}) collective-permute-start(bf16[128,1024]{1,0:T(8,128)(2,1)S(1)} %bitcast.74), channel_id=1, source_target_pairs={{0,2},{1,3},{2,0},{3,1},{4,6},{5,7},{6,4},{7,5},{8,10},{9,11},{10,... | collective-permute-start | bytes 786440 | tf_op jit(solution)/shard_map/ppermute | solution.py:273
  48.0 15.0 %copy-start.10 = (bf16[64,1024]{1,0:T(8,128)(2,1)S(1)}, bf16[64,1024]{1,0:T(8,128)(2,1)}, u32[]{:S(2)}) copy-start(bf16[64,1024]{1,0:T(8,128)(2,1)} %copy-done.9) | copy-start | bytes 393220
  48.0 15.0 %copy-start.12 = (bf16[64,1024]{1,0:T(8,128)(2,1)S(1)}, bf16[64,1024]{1,0:T(8,128)(2,1)}, u32[]{:S(2)}) copy-start(bf16[64,1024]{1,0:T(8,128)(2,1)} %copy-done.11) | copy-start | bytes 393220
  50.6 0.9 copy-start.20
  51.5 8.4 %collective-permute-start.11 = (bf16[512,256]{1,0:T(8,128)(2,1)}, bf16[512,256]{1,0:T(8,128)(2,1)S(1)}, u32[]{:S(2)}, u32[]{:S(2)}) collective-permute-start(bf16[512,256]{1,0:T(8,128)(2,1)} %collective-permute-done.10.refs_2_.refs_1_), channel_id=1, source_target_pairs={{28,0},{0,4},{4,8},{8,12},{12,16},{16,20},{20,24},{24,28},{29,1},{... | collective-permute-start | bytes 786440 | tf_op jit(solution)/shard_map/ppermute | solution.py:269
  51.5 8.5 %collective-permute-start.8 = (bf16[512,256]{1,0:T(8,128)(2,1)}, bf16[512,256]{1,0:T(8,128)(2,1)S(1)}, u32[]{:S(2)}, u32[]{:S(2)}) collective-permute-start(bf16[512,256]{1,0:T(8,128)(2,1)} %collective-permute-done.6.refs_1_.refs_0_), channel_id=1, source_target_pairs={{4,0},{8,4},{12,8},{16,12},{20,16},{24,20},{28,24},{0,28},{5,1},{9... | collective-permute-start | bytes 786440 | tf_op jit(solution)/shard_map/ppermute | solution.py:269
  54.2 8.8 %collective-permute-start.13 = (bf16[128,1024]{1,0:T(8,128)(2,1)S(1)}, bf16[128,1024]{1,0:T(8,128)(2,1)}, u32[]{:S(2)}, u32[]{:S(2)}) collective-permute-start(bf16[128,1024]{1,0:T(8,128)(2,1)S(1)} %bitcast.75), channel_id=1, source_target_pairs={{0,1},{1,0},{2,3},{3,2},{4,5},{5,4},{6,7},{7,6},{8,9},{9,8},{10,11... | collective-permute-start | bytes 786440 | tf_op jit(solution)/shard_map/ppermute | solution.py:273
  55.6 7.5 %collective-permute-start.15 = (bf16[128,1024]{1,0:T(8,128)(2,1)}, bf16[128,1024]{1,0:T(8,128)(2,1)}, u32[]{:S(2)}, u32[]{:S(2)}) collective-permute-start(bf16[128,1024]{1,0:T(8,128)(2,1)} %collective-permute-done.14.refs_2_), channel_id=1, source_target_pairs={{0,1},{1,0},{2,3},{3,2},{4,5},{5,4},{6,7},{7,6},{8,9},{9,8},{10,11... | collective-permute-start | bytes 786440 | tf_op jit(solution)/shard_map/ppermute | solution.py:273
  59.9 8.7 %collective-permute-start.12 = (bf16[256,256]{1,0:T(8,128)(2,1)S(1)}, bf16[256,256]{1,0:T(8,128)(2,1)S(1)}, u32[]{:S(2)}, u32[]{:S(2)}) collective-permute-start(bf16[256,256]{1,0:T(8,128)(2,1)S(1)} %slice.88), channel_id=1, source_target_pairs={{28,0},{0,4},{4,8},{8,12},{12,16},{16,20},{20,24},{24,28},{29,1},{... | collective-permute-start | bytes 393224 | tf_op jit(solution)/shard_map/ppermute | solution.py:269
  60.1 4.6 %copy-start.16 = (s32[4]{0:T(128)S(1)}, s32[4]{0:T(128)}, u32[]{:S(2)}) copy-start(s32[4]{0:T(128)} %constant.73.clone.number_ref) | copy-start | bytes 52
  60.1 4.6 %copy-start.19 = (bf16[512,128]{1,0:T(8,128)(2,1)S(1)}, bf16[512,128]{1,0:T(8,128)(2,1)}, u32[]{:S(2)}) copy-start(bf16[512,128]{1,0:T(8,128)(2,1)} %copy-done.18) | copy-start | bytes 393220
  60.1 4.6 %copy-start.21 = (f32[3,512,128]{2,1,0:T(8,128)S(1)}, f32[3,512,128]{2,1,0:T(8,128)}, u32[]{:S(2)}) copy-start(f32[3,512,128]{2,1,0:T(8,128)} %copy-done.20) | copy-start | bytes 2359300
  60.1 8.6 %collective-permute-start.9 = (bf16[256,256]{1,0:T(8,128)(2,1)S(1)}, bf16[256,256]{1,0:T(8,128)(2,1)S(1)}, u32[]{:S(2)}, u32[]{:S(2)}) collective-permute-start(bf16[256,256]{1,0:T(8,128)(2,1)S(1)} %slice.87), channel_id=1, source_target_pairs={{4,0},{8,4},{12,8},{16,12},{20,16},{24,20},{28,24},{0,28},{5,1},{9... | collective-permute-start | bytes 393224 | tf_op jit(solution)/shard_map/ppermute | solution.py:269
  70.0 1.2 copy-start.15
  73.4 14.8 %collective-permute-start.23 = (bf16[512,128]{1,0:T(8,128)(2,1)S(1)}, bf16[512,128]{1,0:T(8,128)(2,1)S(1)}, u32[]{:S(2)}, u32[]{:S(2)}) collective-permute-start(bf16[512,128]{1,0:T(8,128)(2,1)S(1)} %get-tuple-element.51.a_ref.refs_0_), channel_id=1, source_target_pairs={{0,2},{1,3},{2,0},{3,1},{4,6},{5,7},{6,4},{7,5},{8,10},{9,11},{10,... | collective-permute-start | bytes 393224 | tf_op jit(solution)/shard_map/ppermute | solution.py:273
  76.4 16.3 %collective-permute-start.22 = (bf16[512,128]{1,0:T(8,128)(2,1)S(1)}, bf16[512,128]{1,0:T(8,128)(2,1)S(1)}, u32[]{:S(2)}, u32[]{:S(2)}) collective-permute-start(bf16[512,128]{1,0:T(8,128)(2,1)S(1)} %get-tuple-element.51.a_ref.refs_0_), channel_id=1, source_target_pairs={{0,1},{1,0},{2,3},{3,2},{4,5},{5,4},{6,7},{7,6},{8,9},{9,8},{10,11... | collective-permute-start | bytes 393224 | tf_op jit(solution)/shard_map/ppermute | solution.py:273
  78.8 6.4 %collective-permute-start.18 = (bf16[256,256]{1,0:T(8,128)(2,1)S(1)}, bf16[256,256]{1,0:T(8,128)(2,1)S(1)}, u32[]{:S(2)}, u32[]{:S(2)}) collective-permute-start(bf16[256,256]{1,0:T(8,128)(2,1)S(1)} %get-tuple-element.81), channel_id=1, source_target_pairs={{28,0},{0,4},{4,8},{8,12},{12,16},{16,20},{20,24},{24,28},{29,1},{... | collective-permute-start | bytes 393224 | tf_op jit(solution)/shard_map/ppermute | solution.py:269
  78.9 6.3 %collective-permute-start.20 = (bf16[256,256]{1,0:T(8,128)(2,1)S(1)}, bf16[256,256]{1,0:T(8,128)(2,1)S(1)}, u32[]{:S(2)}, u32[]{:S(2)}) collective-permute-start(bf16[256,256]{1,0:T(8,128)(2,1)S(1)} %get-tuple-element.80), channel_id=1, source_target_pairs={{4,0},{8,4},{12,8},{16,12},{20,16},{24,20},{28,24},{0,28},{5,1},{9... | collective-permute-start | bytes 393224 | tf_op jit(solution)/shard_map/ppermute | solution.py:269
  82.0 18.9 %collective-permute-start.16 = (bf16[2,128,1024]{2,1,0:T(8,128)(2,1)S(1)}, bf16[2,128,1024]{2,1,0:T(8,128)(2,1)S(1)}, u32[]{:S(2)}, u32[]{:S(2)}) collective-permute-start(bf16[2,128,1024]{2,1,0:T(8,128)(2,1)S(1)} %get-tuple-element.54), channel_id=1, source_target_pairs={{0,1},{1,0},{2,3},{3,2},{4,5},{5,4},{6,7},{7,6},{8,9},{9,8},{10,11... | collective-permute-start | bytes 1572872 | tf_op jit(solution)/shard_map/ppermute | solution.py:273
  82.7 6.9 %copy-start.14 = (s32[2]{0:T(128)S(1)}, s32[2]{0:T(128)}, u32[]{:S(2)}) copy-start(s32[2]{0:T(128)} %constant.76.clone.number_ref) | copy-start | bytes 28
  85.3 9.1 %collective-permute-start.19 = (bf16[512,256]{1,0:T(8,128)(2,1)S(1)}, bf16[512,256]{1,0:T(8,128)(2,1)S(1)}, u32[]{:S(2)}, u32[]{:S(2)}) collective-permute-start(bf16[512,256]{1,0:T(8,128)(2,1)S(1)} %pad_maximum_fusion.2), channel_id=1, source_target_pairs={{28,0},{0,4},{4,8},{8,12},{12,16},{16,20},{20,24},{24,28},{29,1},{... | collective-permute-start | bytes 786440 | tf_op jit(solution)/shard_map/ppermute | solution.py:269
  85.5 9.0 %collective-permute-start.21 = (bf16[512,256]{1,0:T(8,128)(2,1)S(1)}, bf16[512,256]{1,0:T(8,128)(2,1)S(1)}, u32[]{:S(2)}, u32[]{:S(2)}) collective-permute-start(bf16[512,256]{1,0:T(8,128)(2,1)S(1)} %pad_maximum_fusion.3), channel_id=1, source_target_pairs={{4,0},{8,4},{12,8},{16,12},{20,16},{24,20},{28,24},{0,28},{5,1},{9... | collective-permute-start | bytes 786440 | tf_op jit(solution)/shard_map/ppermute | solution.py:269
  88.2 4.4 %collective-permute-start.24 = (bf16[512,128]{1,0:T(8,128)(2,1)S(1)}, bf16[512,128]{1,0:T(8,128)(2,1)S(1)}, u32[]{:S(2)}, u32[]{:S(2)}) collective-permute-start(bf16[512,128]{1,0:T(8,128)(2,1)S(1)} %collective-permute-done.23.refs_2_), channel_id=1, source_target_pairs={{0,1},{1,0},{2,3},{3,2},{4,5},{5,4},{6,7},{7,6},{8,9},{9,8},{10,11... | collective-permute-start | bytes 393224 | tf_op jit(solution)/shard_map/ppermute | solution.py:273
  94.4 3.0 %copy-start.4 = (bf16[512,256]{1,0:T(8,128)(2,1)S(1)}, bf16[512,256]{1,0:T(8,128)(2,1)}, u32[]{:S(2)}) copy-start(bf16[512,256]{1,0:T(8,128)(2,1)} %copy-done.3) | copy-start | bytes 786436
  94.4 3.0 %copy-start.6 = (bf16[512,256]{1,0:T(8,128)(2,1)S(1)}, bf16[512,256]{1,0:T(8,128)(2,1)}, u32[]{:S(2)}) copy-start(bf16[512,256]{1,0:T(8,128)(2,1)} %copy-done.5) | copy-start | bytes 786436
  94.4 3.0 %copy-start.8 = (bf16[512,256]{1,0:T(8,128)(2,1)S(1)}, bf16[512,256]{1,0:T(8,128)(2,1)}, u32[]{:S(2)}) copy-start(bf16[512,256]{1,0:T(8,128)(2,1)} %copy-done.7) | copy-start | bytes 786436
  94.4 2.9 %copy-start.13 = (s32[3]{0:T(128)S(1)}, s32[3]{0:T(128)}, u32[]{:S(2)}) copy-start(s32[3]{0:T(128)} %constant.77.clone.number_ref) | copy-start | bytes 40
  94.6 8.2 %collective-permute-start.25 = (bf16[512,256]{1,0:T(8,128)(2,1)S(1)}, bf16[512,256]{1,0:T(8,128)(2,1)S(1)}, u32[]{:S(2)}, u32[]{:S(2)}) collective-permute-start(bf16[512,256]{1,0:T(8,128)(2,1)S(1)} %get-tuple-element.75), channel_id=1, source_target_pairs={{28,0},{0,4},{4,8},{8,12},{12,16},{16,20},{20,24},{24,28},{29,1},{... | collective-permute-start | bytes 786440 | tf_op jit(solution)/shard_map/ppermute | solution.py:269
  95.4 7.3 %collective-permute-start.27 = (bf16[512,256]{1,0:T(8,128)(2,1)S(1)}, bf16[512,256]{1,0:T(8,128)(2,1)S(1)}, u32[]{:S(2)}, u32[]{:S(2)}) collective-permute-start(bf16[512,256]{1,0:T(8,128)(2,1)S(1)} %get-tuple-element.74), channel_id=1, source_target_pairs={{4,0},{8,4},{12,8},{16,12},{20,16},{24,20},{28,24},{0,28},{5,1},{9... | collective-permute-start | bytes 786440 | tf_op jit(solution)/shard_map/ppermute | solution.py:269
  101.1 6.3 %collective-permute-start.17 = (bf16[128,1024]{1,0:T(8,128)(2,1)S(1)}, bf16[128,1024]{1,0:T(8,128)(2,1)S(1)}, u32[]{:S(2)}, u32[]{:S(2)}) collective-permute-start(bf16[128,1024]{1,0:T(8,128)(2,1)S(1)} %get-tuple-element.56), channel_id=1, source_target_pairs={{0,2},{1,3},{2,0},{3,1},{4,6},{5,7},{6,4},{7,5},{8,10},{9,11},{10,... | collective-permute-start | bytes 786440 | tf_op jit(solution)/shard_map/ppermute | solution.py:273
  102.9 7.3 %collective-permute-start.26 = (bf16[512,256]{1,0:T(8,128)(2,1)S(1)}, bf16[512,256]{1,0:T(8,128)(2,1)S(1)}, u32[]{:S(2)}, u32[]{:S(2)}) collective-permute-start(bf16[512,256]{1,0:T(8,128)(2,1)S(1)} %get-tuple-element.72), channel_id=1, source_target_pairs={{28,0},{0,4},{4,8},{8,12},{12,16},{16,20},{20,24},{24,28},{29,1},{... | collective-permute-start | bytes 786440 | tf_op jit(solution)/shard_map/ppermute | solution.py:269
  103.0 7.2 %collective-permute-start.28 = (bf16[512,256]{1,0:T(8,128)(2,1)S(1)}, bf16[512,256]{1,0:T(8,128)(2,1)S(1)}, u32[]{:S(2)}, u32[]{:S(2)}) collective-permute-start(bf16[512,256]{1,0:T(8,128)(2,1)S(1)} %get-tuple-element.73), channel_id=1, source_target_pairs={{4,0},{8,4},{12,8},{16,12},{20,16},{24,20},{28,24},{0,28},{5,1},{9... | collective-permute-start | bytes 786440 | tf_op jit(solution)/shard_map/ppermute | solution.py:269
  111.9 15.6 %all-to-all-start.1 = ((bf16[8,128,512]{2,1,0:T(8,128)(2,1)}), bf16[8,128,512]{2,1,0:T(8,128)(2,1)S(1)}, u32[]{:S(2)}, u32[]{:S(2)}) async-start(bf16[8,128,512]{2,1,0:T(8,128)(2,1)} %pad_maximum_fusion), calls=%async_computation.1 | async-start | bytes 2097152 | tf_op jit(solution)/shard_map/all_to_all | solution.py:314
  116.3 4.4 %collective-permute-start.29 = (bf16[2,128,1024]{2,1,0:T(8,128)(2,1)S(1)}, bf16[2,128,1024]{2,1,0:T(8,128)(2,1)S(1)}, u32[]{:S(2)}, u32[]{:S(2)}) collective-permute-start(bf16[2,128,1024]{2,1,0:T(8,128)(2,1)S(1)} %get-tuple-element.68), channel_id=1, source_target_pairs={{0,1},{1,0},{2,3},{3,2},{4,5},{5,4},{6,7},{7,6},{8,9},{9,8},{10,11... | collective-permute-start | bytes 1572872 | tf_op jit(solution)/shard_map/ppermute | solution.py:273
  120.8 20.1 %collective-permute-start.30 = (bf16[128,1024]{1,0:T(8,128)(2,1)S(1)}, bf16[128,1024]{1,0:T(8,128)(2,1)S(1)}, u32[]{:S(2)}, u32[]{:S(2)}) collective-permute-start(bf16[128,1024]{1,0:T(8,128)(2,1)S(1)} %get-tuple-element.70), channel_id=1, source_target_pairs={{0,2},{1,3},{2,0},{3,1},{4,6},{5,7},{6,4},{7,5},{8,10},{9,11},{10,... | collective-permute-start | bytes 786440 | tf_op jit(solution)/shard_map/ppermute | solution.py:273
  128.3 21.7 %all-to-all-start.2 = ((bf16[32,4,512]{2,1,0:T(4,128)(2,1)}), bf16[32,4,512]{2,1,0:T(4,128)(2,1)S(1)}, u32[]{:S(2)}, u32[]{:S(2)}) async-start(bf16[32,4,512]{2,1,0:T(4,128)(2,1)} %clips_sum.1), calls=%async_computation.2 | async-start | bytes 262144 | tf_op jit(solution)/shard_map/all_to_all | solution.py:314

commit v2 on v1

--- a/solution.py
+++ b/solution.py
@@ -399,6 +399,18 @@
     )
     kv_ring = Ring(kv)
     kv_ring.step()
+    dy_near = gather(after(dy_own, kv))
+    g, dy, out_head = call(
+        cotangent_kernel,
+        "cotangent",
+        (head_rows, model_rows, jax.ShapeDtypeStruct((HD, 1024), BF)),
+        [],
+        2 * work,
+        lax.axis_index("f").reshape(1),
+        *halves,
+        *dy_near,
+    )
+
     def forward(number, state, *more, q=q):
         at_once = 1
         pieces = kv_ring.pieces(number)
@@ -425,19 +437,8 @@
             there=range(2, 2 + len(pieces)),
         )
 
-    dy_near = gather(after(dy_own, *kv_ring.blocks[1], *kv_ring.blocks[7]))
-    g, dy, out_head = call(
-        cotangent_kernel,
-        "cotangent",
-        (head_rows, model_rows, jax.ShapeDtypeStruct((HD, 1024), BF)),
-        [],
-        2 * work,
-        lax.axis_index("f").reshape(1),
-        *halves,
-        *dy_near,
-    )
     kv_ring.step()
-    state = (forward((0, 1, 7), ()),)
+    state = (forward((0, 1, 7), (), q=after(q, *dy_near)),)
     kv_ring.step(*state)
     kv_ring.step()
     state = (forward((2, 6, 3, 5), state),)
@@ -474,7 +475,6 @@
     up = take(part[0, :half], "z", NZ, -1)
     down = take(part[0, half:], "z", NZ, 1)
     part, acc = backward((3, 5), (acc,))
-    sent = acc
     up = jnp.concatenate([add(part[0, :half], up), part[0, half:]], axis=0)
     down = jnp.concatenate([part[1, :half], add(part[1, half:], down)], axis=0)
     up, down = take(up, "z", NZ, -1), take(down, "z", NZ, 1)
@@ -499,7 +499,7 @@
         ],
         2 * work,
         h.reshape(1),
-        *gather(after(att, sent)),
+        *gather(att),
         dy,
         there=range(1, HEADS + 2),
     )
@@ -520,7 +520,7 @@
     )
     d_head = jnp.concatenate([after(dkv, terms), dq], axis=1)
     token_grad = heads_terms(d_head, w_head, True)
-    token_grad = (dy_own.astype(F32) + add_heads(*token_grad)).astype(BF)
+    token_grad = (dy_own.astype(F32) + add_heads(*token_grad, got)).astype(BF)
 
     sums = after(exchange(got, ("z", "h")), token_grad).reshape(NZ, HEADS, 4, 4 * HD)
     sums = jnp.sum(sums.astype(F32), axis=0)

time: 152 us -> 149 us (0.980)
  waiting for transfers between devices: 41.3 us -> 34.4 us
  local copies, waits for them, and re-layouts: 5.54 us -> 11.4 us
    ppermute x16, waiting for transfers between devices: 16.8 us -> 9.23 us  [take(): return lax.ppermute(x, axis, [((i + by) % size, i) for i in range(size)])]
    unnamed x48 -> x60, local copies, waits for them, and re-layouts: 1.05 us -> 6.9 us
  transfers between devices with their start and end apart: 34 -> 34, of which waited for: 10 -> 11; matrix products, arithmetic and copies ran while one was open for 4% -> 4% of each run, Pallas kernels for 12% -> 13%
where the time goes in v2:
time: 149 us; the launch traced here: 148 us
  starting transfers between devices  73.9 us (50%)
  waiting for transfers between devices  34.4 us (23%)
  Pallas kernels  22.5 us (15%)
  local copies, waits for them, and re-layouts  11.4 us (8%)
  other arithmetic  3.36 us (2%)
    ppermute x16, starting transfers between devices, take(): return lax.ppermute(x, axis, [((i + by) % size, i) for i in range(size)])  25.4 us
    pallas_call x16, Pallas kernels, call(): pl.pallas_call(kernel, name=name, out_shape=out_shape, in_specs=specs, ou...  22.5 us
    all_to_all x3, starting transfers between devices, exchange(): return lax.all_to_all(x, axis, split_axis=0, concat_axis=0, tiled=True)  21.5 us
    ppermute x13, starting transfers between devices, swap(): return lax.ppermute(x, 'h', [(i, i ^ bit) for i in range(HEADS)])  20.1 us
    all_to_all x3, waiting for transfers between devices, exchange(): return lax.all_to_all(x, axis, split_axis=0, concat_axis=0, tiled=True)  15.1 us
    ppermute x16, waiting for transfers between devices, take(): return lax.ppermute(x, axis, [((i + by) % size, i) for i in range(size)])  9.23 us
    unnamed x60, local copies, waits for them, and re-layouts  6.9 us
    ppermute x2, starting transfers between devices, half_of_head(): return lax.ppermute(after(w_out, x_near[2]), ('f', 'h'), pairs)  6.84 us
  transfers between devices with their start and end apart: 34, of which 11 were waited for; matrix products, arithmetic and copies ran while one was open for 4% of the time, Pallas kernels for 13%

profile of v2, /device:TPU:1, one launch (start us, length us, event | category | flops | bytes accessed | tf_op | source)
XLA Modules:
  0.0 148.0 jit_solution(4179304515629285887)
XLA Ops:
  0.6 2.1 %collective-permute-start.1 = (bf16[128,1024]{1,0:T(8,128)(2,1)}, bf16[128,1024]{1,0:T(8,128)(2,1)S(1)}, u32[]{:S(2)}, u32[]{:S(2)}) collective-permute-start(bf16[128,1024]{1,0:T(8,128)(2,1)} %bitcast.69), channel_id=1, source_target_pairs={{0,2},{1,3},{2,0},{3,1},{4,6},{5,7},{6,4},{7,5},{8,10},{9,11},{10,... | collective-permute-start | bytes 786440 | tf_op jit(solution)/shard_map/ppermute | solution.py:273
  2.8 1.3 collective-permute-start
  4.1 0.8 constant_dynamic-slice_fusion.1
  4.9 1.0 broadcast_in_dim.33
  5.9 6.1 %all-to-all-start = ((bf16[8,128,384]{2,1,0:T(8,128)(2,1)}), bf16[8,128,384]{2,1,0:T(8,128)(2,1)S(1)}, u32[]{:S(2)}, u32[]{:S(2)}) async-start(bf16[8,128,384]{2,1,0:T(8,128)(2,1)} %broadcast_in_dim.33), calls=%async_computation | async-start | bytes 1572864 | tf_op jit(solution)/shard_map/all_to_all | solution.py:314
  13.4 3.5 %collective-permute-start.3 = (bf16[64,1024]{1,0:T(8,128)(2,1)}, bf16[64,1024]{1,0:T(8,128)(2,1)S(1)}, u32[]{:S(2)}, u32[]{:S(2)}) collective-permute-start(bf16[64,1024]{1,0:T(8,128)(2,1)} %param.20), channel_id=1, source_target_pairs={{0,0},{64,1},{128,2},{192,3},{1,32},{65,33},{129,34},{193,35},{2,6... | collective-permute-start | bytes 393224 | tf_op jit(solution)/shard_map/ppermute | solution.py:385
  17.0 3.3 %collective-permute-start.4 = (bf16[64,1024]{1,0:T(8,128)(2,1)}, bf16[64,1024]{1,0:T(8,128)(2,1)S(1)}, u32[]{:S(2)}, u32[]{:S(2)}) collective-permute-start(bf16[64,1024]{1,0:T(8,128)(2,1)} %param.20), channel_id=1, source_target_pairs={{32,0},{96,1},{160,2},{224,3},{33,32},{97,33},{161,34},{225,35},{3... | collective-permute-start | bytes 393224 | tf_op jit(solution)/shard_map/ppermute | solution.py:385
  21.2 6.2 %collective-permute-done.3.a_ref = bf16[64,1024]{1,0:T(8,128)(2,1)S(1)} collective-permute-done((bf16[64,1024]{1,0:T(8,128)(2,1)}, bf16[64,1024]{1,0:T(8,128)(2,1)S(1)}, u32[]{:S(2)}, u32[]{:S(2)}) %collective-permute-start.3) | collective-permute-done | bytes 131104 | tf_op jit(solution)/shard_map/ppermute | solution.py:385
  27.5 0.7 tokens.1
  28.5 5.3 %collective-permute-start.8 = (bf16[128,1024]{1,0:T(8,128)(2,1)S(1)}, bf16[128,1024]{1,0:T(8,128)(2,1)S(1)}, u32[]{:S(2)}, u32[]{:S(2)}) collective-permute-start(bf16[128,1024]{1,0:T(8,128)(2,1)S(1)} %bitcast.74), channel_id=1, source_target_pairs={{0,2},{1,3},{2,0},{3,1},{4,6},{5,7},{6,4},{7,5},{8,10},{9,11},{10,... | collective-permute-start | bytes 786440 | tf_op jit(solution)/shard_map/ppermute | solution.py:273
  33.8 1.6 %collective-permute-start.10 = (bf16[512,256]{1,0:T(8,128)(2,1)S(1)}, bf16[512,256]{1,0:T(8,128)(2,1)S(1)}, u32[]{:S(2)}, u32[]{:S(2)}) collective-permute-start(bf16[512,256]{1,0:T(8,128)(2,1)S(1)} %get-tuple-element.44.refs_1_.refs_2_), channel_id=1, source_target_pairs={{28,0},{0,4},{4,8},{8,12},{12,16},{16,20},{20,24},{24,28},{29,1},{... | collective-permute-start | bytes 786440 | tf_op jit(solution)/shard_map/ppermute | solution.py:269
  35.4 3.9 %collective-permute-start.5 = (bf16[512,256]{1,0:T(8,128)(2,1)S(1)}, bf16[512,256]{1,0:T(8,128)(2,1)S(1)}, u32[]{:S(2)}, u32[]{:S(2)}) collective-permute-start(bf16[512,256]{1,0:T(8,128)(2,1)S(1)} %get-tuple-element.44.refs_1_.refs_2_), channel_id=1, source_target_pairs={{4,0},{8,4},{12,8},{16,12},{20,16},{24,20},{28,24},{0,28},{5,1},{9... | collective-permute-start | bytes 786440 | tf_op jit(solution)/shard_map/ppermute | solution.py:269
  39.4 0.5 collective-permute-done.8.refs_2_
  39.9 0.7 copy-done.9
  40.6 4.8 %collective-permute-done.10.refs_3_.refs_1_ = bf16[512,256]{1,0:T(8,128)(2,1)S(1)} collective-permute-done((bf16[512,256]{1,0:T(8,128)(2,1)S(1)}, bf16[512,256]{1,0:T(8,128)(2,1)S(1)}, u32[]{:S(2)}, u32[]{:S(2)}) %collective-permute-start.10) | collective-permute-done | bytes 262176 | tf_op jit(solution)/shard_map/ppermute | solution.py:269
  45.4 3.0 %collective-permute-start.6 = (bf16[512,256]{1,0:T(8,128)(2,1)S(1)}, bf16[512,256]{1,0:T(8,128)(2,1)}, u32[]{:S(2)}, u32[]{:S(2)}) collective-permute-start(bf16[512,256]{1,0:T(8,128)(2,1)S(1)} %collective-permute-done.5.refs_2_.refs_0_), channel_id=1, source_target_pairs={{4,0},{8,4},{12,8},{16,12},{20,16},{24,20},{28,24},{0,28},{5,1},{9... | collective-permute-start | bytes 786440 | tf_op jit(solution)/shard_map/ppermute | solution.py:269
  48.4 0.7 copy-done.11
  49.1 0.7 copy-done.13
  49.8 2.5 %attn_forward.2.refs_6_ = f32[3,512,128]{2,1,0:T(8,128)S(1)} custom-call(s32[3]{0:T(128)S(1)} %copy-done.23, bf16[512,128]{1,0:T(8,128)(2,1)S(1)} %get-tuple-element.46.refs_0_.q_ref, bf16[512,256]{1,0:T(8,128)(2,1)S(1)} %get-tuple-element.44.refs_1_.refs_2_, bf16[512,256]{1,0:T(8,128)(2,1)S(1)} %collective-permute-done.5.refs_2_.refs_0_, ...), custom_call_target="tpu_custom_call" | custom-call | flops 1610612736 | bytes 1048576 | tf_op jit(solution)/shard_map/attn_forward/pallas_call | solution.py:254
  52.3 0.6 copy-done.24
  53.0 0.9 copy-done.26
  53.9 0.5 collective-permute-done.13.refs_2_.refs_1_
  54.4 2.8 %collective-permute-start.11 = (bf16[512,256]{1,0:T(8,128)(2,1)}, bf16[512,256]{1,0:T(8,128)(2,1)S(1)}, u32[]{:S(2)}, u32[]{:S(2)}) collective-permute-start(bf16[512,256]{1,0:T(8,128)(2,1)} %collective-permute-done.6.refs_1_.refs_0_), channel_id=1, source_target_pairs={{4,0},{8,4},{12,8},{16,12},{20,16},{24,20},{28,24},{0,28},{5,1},{9... | collective-permute-start | bytes 786440 | tf_op jit(solution)/shard_map/ppermute | solution.py:269
  57.2 0.9 copy-done.10
  58.2 0.9 copy-done.12
  59.1 0.9 copy-done.14
  60.1 0.5 cotangent.1
  60.6 2.0 %collective-permute-done.14.refs_4_.refs_1_ = bf16[512,256]{1,0:T(8,128)(2,1)S(1)} collective-permute-done((bf16[512,256]{1,0:T(8,128)(2,1)}, bf16[512,256]{1,0:T(8,128)(2,1)S(1)}, u32[]{:S(2)}, u32[]{:S(2)}) %collective-permute-start.14) | collective-permute-done | bytes 262176 | tf_op jit(solution)/shard_map/ppermute | solution.py:269
  62.9 2.7 %collective-permute-start.12 = (bf16[256,256]{1,0:T(8,128)(2,1)S(1)}, bf16[256,256]{1,0:T(8,128)(2,1)S(1)}, u32[]{:S(2)}, u32[]{:S(2)}) collective-permute-start(bf16[256,256]{1,0:T(8,128)(2,1)S(1)} %slice.87), channel_id=1, source_target_pairs={{4,0},{8,4},{12,8},{16,12},{20,16},{24,20},{28,24},{0,28},{5,1},{9... | collective-permute-start | bytes 393224 | tf_op jit(solution)/shard_map/ppermute | solution.py:269
  65.6 4.0 %attn_forward.3.refs_4_ = f32[3,512,128]{2,1,0:T(8,128)S(1)} custom-call(s32[4]{0:T(128)S(1)} %copy-done.22, bf16[512,128]{1,0:T(8,128)(2,1)S(1)} %copy-done.25, bf16[512,256]{1,0:T(8,128)(2,1)} %collective-permute-done.6.refs_1_.refs_0_, bf16[512,256]{1,0:T(8,128)(2,1)} %collective-permute-done.13.refs_2_.refs_1_, ...), custom_call_target="tpu_custom_call" | custom-call | flops 2147483648 | bytes 1048576 | tf_op jit(solution)/shard_map/attn_forward/pallas_call | solution.py:254
  69.6 1.3 attn_forward_end.1
  71.0 2.6 %collective-permute-start.22 = (bf16[512,128]{1,0:T(8,128)(2,1)S(1)}, bf16[512,128]{1,0:T(8,128)(2,1)S(1)}, u32[]{:S(2)}, u32[]{:S(2)}) collective-permute-start(bf16[512,128]{1,0:T(8,128)(2,1)S(1)} %get-tuple-element.54.a_ref.refs_0_), channel_id=1, source_target_pairs={{0,1},{1,0},{2,3},{3,2},{4,5},{5,4},{6,7},{7,6},{8,9},{9,8},{10,11... | collective-permute-start | bytes 393224 | tf_op jit(solution)/shard_map/ppermute | solution.py:273
  73.6 1.1 attn_backward.4
  74.9 2.7 %collective-permute-start.20 = (bf16[256,256]{1,0:T(8,128)(2,1)S(1)}, bf16[256,256]{1,0:T(8,128)(2,1)S(1)}, u32[]{:S(2)}, u32[]{:S(2)}) collective-permute-start(bf16[256,256]{1,0:T(8,128)(2,1)S(1)} %get-tuple-element.84), channel_id=1, source_target_pairs={{4,0},{8,4},{12,8},{16,12},{20,16},{24,20},{28,24},{0,28},{5,1},{9... | collective-permute-start | bytes 393224 | tf_op jit(solution)/shard_map/ppermute | solution.py:269
  77.6 2.2 %attn_backward.5 = (bf16[2,512,256]{2,1,0:T(8,128)(2,1)S(1)}, f32[128,512]{1,0:T(8,128)S(1)}) custom-call(bf16[512,128]{1,0:T(8,128)(2,1)S(1)} %copy-done.25, bf16[512,128]{1,0:T(8,128)(2,1)S(1)} %get-tuple-element.49.refs_5_.g_ref, f32[2,512]{1,0:T(2,128)S(1)} %get-tuple-element.51.stat_ref, s32[2]{0:T(128)S(1)} %copy-done.21, ...), custom_call_target="tpu_custom_call" | custom-call | flops 2684354560 | bytes 1048576 | tf_op jit(solution)/shard_map/attn_backward/pallas_call | solution.py:254
  80.2 0.7 collective-permute-start.16
  81.3 1.6 %collective-permute-start.19 = (bf16[512,256]{1,0:T(8,128)(2,1)S(1)}, bf16[512,256]{1,0:T(8,128)(2,1)S(1)}, u32[]{:S(2)}, u32[]{:S(2)}) collective-permute-start(bf16[512,256]{1,0:T(8,128)(2,1)S(1)} %pad_maximum_fusion.2), channel_id=1, source_target_pairs={{28,0},{0,4},{4,8},{8,12},{12,16},{16,20},{20,24},{24,28},{29,1},{... | collective-permute-start | bytes 786440 | tf_op jit(solution)/shard_map/ppermute | solution.py:269
  82.9 1.3 collective-permute-start.21
  84.1 1.4 collective-permute-start.24
  85.5 3.1 %attn_backward.6 = (bf16[2,512,256]{2,1,0:T(8,128)(2,1)S(1)}, f32[128,512]{1,0:T(8,128)S(1)}) custom-call(bf16[512,128]{1,0:T(8,128)(2,1)S(1)} %copy-done.25, bf16[512,128]{1,0:T(8,128)(2,1)S(1)} %get-tuple-element.49.refs_5_.g_ref, f32[2,512]{1,0:T(2,128)S(1)} %get-tuple-element.51.stat_ref, s32[2]{0:T(128)S(1)} %copy-done.20, ...), custom_call_target="tpu_custom_call" | custom-call | flops 2684354560 | bytes 1048576 | tf_op jit(solution)/shard_map/attn_backward/pallas_call | solution.py:254
  88.7 1.7 %grad_out.1 = bf16[8,128,128]{2,1,0:T(8,128)(2,1)S(1)} custom-call(s32[1]{0:T(128)} %bitcast.18.h_ref, bf16[512,128]{1,0:T(8,128)(2,1)S(1)} %get-tuple-element.54.a_ref.refs_0_, bf16[512,128]{1,0:T(8,128)(2,1)S(1)} %collective-permute-done.22.refs_1_, bf16[512,128]{1,0:T(8,128)(2,1)S(1)} %collective-permute-done.23.refs_2_, ...), custom_call_target="tpu_custom_call" | custom-call | flops 536870912 | bytes 1048576 | tf_op jit(solution)/shard_map/grad_out/pallas_call | solution.py:254
  90.6 0.9 collective-permute-start.25
  91.5 1.8 %collective-permute-start.27 = (bf16[512,256]{1,0:T(8,128)(2,1)S(1)}, bf16[512,256]{1,0:T(8,128)(2,1)S(1)}, u32[]{:S(2)}, u32[]{:S(2)}) collective-permute-start(bf16[512,256]{1,0:T(8,128)(2,1)S(1)} %get-tuple-element.78), channel_id=1, source_target_pairs={{4,0},{8,4},{12,8},{16,12},{20,16},{24,20},{28,24},{0,28},{5,1},{9... | collective-permute-start | bytes 786440 | tf_op jit(solution)/shard_map/ppermute | solution.py:269
  93.4 3.1 %attn_backward.7 = (bf16[3,512,256]{2,1,0:T(8,128)(2,1)S(1)}, bf16[512,128]{1,0:T(8,128)(2,1)S(1)}) custom-call(bf16[512,128]{1,0:T(8,128)(2,1)S(1)} %copy-done.25, bf16[512,128]{1,0:T(8,128)(2,1)S(1)} %get-tuple-element.49.refs_5_.g_ref, f32[2,512]{1,0:T(2,128)S(1)} %get-tuple-element.51.stat_ref, s32[3]{0:T(128)S(1)} %copy-done.19, ...), custom_call_target="tpu_custom_call" | custom-call | flops 4026531840 | bytes 1048576 | tf_op jit(solution)/shard_map/attn_backward/pallas_call | solution.py:254
  96.5 0.5 convolution_convert_fusion.1
  97.1 1.7 %collective-permute-start.17 = (bf16[128,1024]{1,0:T(8,128)(2,1)S(1)}, bf16[128,1024]{1,0:T(8,128)(2,1)S(1)}, u32[]{:S(2)}, u32[]{:S(2)}) collective-permute-start(bf16[128,1024]{1,0:T(8,128)(2,1)S(1)} %get-tuple-element.59), channel_id=1, source_target_pairs={{0,2},{1,3},{2,0},{3,1},{4,6},{5,7},{6,4},{7,5},{8,10},{9,11},{10,... | collective-permute-start | bytes 786440 | tf_op jit(solution)/shard_map/ppermute | solution.py:273
  99.1 2.7 %collective-permute-start.28 = (bf16[512,256]{1,0:T(8,128)(2,1)S(1)}, bf16[512,256]{1,0:T(8,128)(2,1)S(1)}, u32[]{:S(2)}, u32[]{:S(2)}) collective-permute-start(bf16[512,256]{1,0:T(8,128)(2,1)S(1)} %get-tuple-element.77), channel_id=1, source_target_pairs={{4,0},{8,4},{12,8},{16,12},{20,16},{24,20},{28,24},{0,28},{5,1},{9... | collective-permute-start | bytes 786440 | tf_op jit(solution)/shard_map/ppermute | solution.py:269
  101.8 1.8 %collective-permute-done.17 = bf16[128,1024]{1,0:T(8,128)(2,1)S(1)} collective-permute-done((bf16[128,1024]{1,0:T(8,128)(2,1)S(1)}, bf16[128,1024]{1,0:T(8,128)(2,1)S(1)}, u32[]{:S(2)}, u32[]{:S(2)}) %collective-permute-start.17) | collective-permute-done | bytes 262176 | tf_op jit(solution)/shard_map/ppermute | solution.py:273
  103.6 0.8 add_convert_fusion.2
  104.4 1.6 %collective-permute-done.26 = bf16[512,256]{1,0:T(8,128)(2,1)S(1)} collective-permute-done((bf16[512,256]{1,0:T(8,128)(2,1)S(1)}, bf16[512,256]{1,0:T(8,128)(2,1)S(1)}, u32[]{:S(2)}, u32[]{:S(2)}) %collective-permute-start.26) | collective-permute-done | bytes 262176 | tf_op jit(solution)/shard_map/ppermute | solution.py:269
  106.1 0.5 convolution_convert_fusion
  106.6 1.1 pad_maximum_fusion
  107.7 3.7 %all-to-all-start.1 = ((bf16[8,128,512]{2,1,0:T(8,128)(2,1)}), bf16[8,128,512]{2,1,0:T(8,128)(2,1)S(1)}, u32[]{:S(2)}, u32[]{:S(2)}) async-start(bf16[8,128,512]{2,1,0:T(8,128)(2,1)} %pad_maximum_fusion), calls=%async_computation.1 | async-start | bytes 2097152 | tf_op jit(solution)/shard_map/all_to_all | solution.py:314
  111.5 0.7 heads_terms.3
  112.2 3.1 %collective-permute-start.29 = (bf16[2,128,1024]{2,1,0:T(8,128)(2,1)S(1)}, bf16[2,128,1024]{2,1,0:T(8,128)(2,1)S(1)}, u32[]{:S(2)}, u32[]{:S(2)}) collective-permute-start(bf16[2,128,1024]{2,1,0:T(8,128)(2,1)S(1)} %get-tuple-element.71), channel_id=1, source_target_pairs={{0,1},{1,0},{2,3},{3,2},{4,5},{5,4},{6,7},{7,6},{8,9},{9,8},{10,11... | collective-permute-start | bytes 1572872 | tf_op jit(solution)/shard_map/ppermute | solution.py:273
  115.3 1.5 %collective-permute-done.29.got_ref = bf16[2,128,1024]{2,1,0:T(8,128)(2,1)S(1)} collective-permute-done((bf16[2,128,1024]{2,1,0:T(8,128)(2,1)S(1)}, bf16[2,128,1024]{2,1,0:T(8,128)(2,1)S(1)}, u32[]{:S(2)}, u32[]{:S(2)}) %collective-permute-start.29) | collective-permute-done | bytes 524320 | tf_op jit(solution)/shard_map/ppermute | solution.py:273
  116.9 6.6 %all-to-all-done.1.got_ref = bf16[8,128,512]{2,1,0:T(8,128)(2,1)S(1)} async-done(((bf16[8,128,512]{2,1,0:T(8,128)(2,1)}), bf16[8,128,512]{2,1,0:T(8,128)(2,1)S(1)}, u32[]{:S(2)}, u32[]{:S(2)}) %all-to-all-start.1) | async-done | bytes 1048608 | tf_op jit(solution)/shard_map/all_to_all | solution.py:314
  123.5 0.8 clips_sum.1
  124.4 1.4 collective-permute-start.30
  125.8 11.7 %all-to-all-start.2 = ((bf16[32,4,512]{2,1,0:T(4,128)(2,1)}), bf16[32,4,512]{2,1,0:T(4,128)(2,1)S(1)}, u32[]{:S(2)}, u32[]{:S(2)}) async-start(bf16[32,4,512]{2,1,0:T(4,128)(2,1)} %clips_sum.1), calls=%async_computation.2 | async-start | bytes 262144 | tf_op jit(solution)/shard_map/all_to_all | solution.py:314
  137.5 0.8 add_convert_fusion
  138.3 8.4 %all-to-all-done.2 = bf16[32,4,512]{2,1,0:T(4,128)(2,1)S(1)} async-done(((bf16[32,4,512]{2,1,0:T(4,128)(2,1)}), bf16[32,4,512]{2,1,0:T(4,128)(2,1)S(1)}, u32[]{:S(2)}, u32[]{:S(2)}) %all-to-all-start.2) | async-done | bytes 131104 | tf_op jit(solution)/shard_map/all_to_all | solution.py:314
  146.8 0.6 slice.93
  147.4 0.6 slice_bitcast_fusion.6
  (124 shorter events, 4.7 us)
Async XLA Ops:
  0.6 3.4 %copy-start = (bf16[128,512]{1,0:T(8,128)(2,1)S(1)}, bf16[128,512]{1,0:T(8,128)(2,1)}, u32[]{:S(2)}) copy-start(bf16[128,512]{1,0:T(8,128)(2,1)} %param.18) | copy-start | bytes 393220
  0.6 12.1 %collective-permute-start.1 = (bf16[128,1024]{1,0:T(8,128)(2,1)}, bf16[128,1024]{1,0:T(8,128)(2,1)S(1)}, u32[]{:S(2)}, u32[]{:S(2)}) collective-permute-start(bf16[128,1024]{1,0:T(8,128)(2,1)} %bitcast.69), channel_id=1, source_target_pairs={{0,2},{1,3},{2,0},{3,1},{4,6},{5,7},{6,4},{7,5},{8,10},{9,11},{10,... | collective-permute-start | bytes 786440 | tf_op jit(solution)/shard_map/ppermute | solution.py:273
  2.8 18.3 %collective-permute-start = (bf16[128,1024]{1,0:T(8,128)(2,1)}, bf16[128,1024]{1,0:T(8,128)(2,1)S(1)}, u32[]{:S(2)}, u32[]{:S(2)}) collective-permute-start(bf16[128,1024]{1,0:T(8,128)(2,1)} %bitcast.70), channel_id=1, source_target_pairs={{0,1},{1,0},{2,3},{3,2},{4,5},{5,4},{6,7},{7,6},{8,9},{9,8},{10,11... | collective-permute-start | bytes 786440 | tf_op jit(solution)/shard_map/ppermute | solution.py:273
  4.9 7.2 %copy-start.28 = (s32[64]{0:T(128)S(1)}, s32[64]{0:T(128)}, u32[]{:S(2)}) copy-start(s32[64]{0:T(128)} %param.22) | copy-start | bytes 772
  5.9 7.2 %copy-start.29 = (s32[32,32]{1,0:T(8,128)S(1)}, s32[32,32]{1,0:T(8,128)}, u32[]{:S(2)}) copy-start(s32[32,32]{1,0:T(8,128)} %param.21) | copy-start | bytes 12292
  5.9 21.6 %all-to-all-start = ((bf16[8,128,384]{2,1,0:T(8,128)(2,1)}), bf16[8,128,384]{2,1,0:T(8,128)(2,1)S(1)}, u32[]{:S(2)}, u32[]{:S(2)}) async-start(bf16[8,128,384]{2,1,0:T(8,128)(2,1)} %broadcast_in_dim.33), calls=%async_computation | async-start | bytes 1572864 | tf_op jit(solution)/shard_map/all_to_all | solution.py:314
  12.0 9.1 %copy-start.1 = (bf16[1,128,1024]{2,1,0:T(8,128)(2,1)S(1)}, bf16[1,128,1024]{2,1,0:T(8,128)(2,1)}, u32[]{:S(2)}) copy-start(bf16[1,128,1024]{2,1,0:T(8,128)(2,1)} %param.15) | copy-start | bytes 786436
  12.8 8.3 %collective-permute-start.2 = (bf16[128,1024]{1,0:T(8,128)(2,1)S(1)}, bf16[128,1024]{1,0:T(8,128)(2,1)S(1)}, u32[]{:S(2)}, u32[]{:S(2)}) collective-permute-start(bf16[128,1024]{1,0:T(8,128)(2,1)S(1)} %collective-permute-done.1.refs_2_), channel_id=1, source_target_pairs={{0,1},{1,0},{2,3},{3,2},{4,5},{5,4},{6,7},{7,6},{8,9},{9,8},{10,11... | collective-permute-start | bytes 786440 | tf_op jit(solution)/shard_map/ppermute | solution.py:273
  13.4 14.0 %collective-permute-start.3 = (bf16[64,1024]{1,0:T(8,128)(2,1)}, bf16[64,1024]{1,0:T(8,128)(2,1)S(1)}, u32[]{:S(2)}, u32[]{:S(2)}) collective-permute-start(bf16[64,1024]{1,0:T(8,128)(2,1)} %param.20), channel_id=1, source_target_pairs={{0,0},{64,1},{128,2},{192,3},{1,32},{65,33},{129,34},{193,35},{2,6... | collective-permute-start | bytes 393224 | tf_op jit(solution)/shard_map/ppermute | solution.py:385
  17.0 10.5 %collective-permute-start.4 = (bf16[64,1024]{1,0:T(8,128)(2,1)}, bf16[64,1024]{1,0:T(8,128)(2,1)S(1)}, u32[]{:S(2)}, u32[]{:S(2)}) collective-permute-start(bf16[64,1024]{1,0:T(8,128)(2,1)} %param.20), channel_id=1, source_target_pairs={{32,0},{96,1},{160,2},{224,3},{33,32},{97,33},{161,34},{225,35},{3... | collective-permute-start | bytes 393224 | tf_op jit(solution)/shard_map/ppermute | solution.py:385
  27.4 0.8 copy-start.15
  27.4 0.8 copy-start.17
  27.5 1.0 copy-start.2
  27.5 22.3 %copy-start.23 = (s32[3]{0:T(128)S(1)}, s32[3]{0:T(128)}, u32[]{:S(2)}) copy-start(s32[3]{0:T(128)} %constant.72.clone.number_ref) | copy-start | bytes 40
  28.2 24.1 %copy-start.3 = (bf16[512,256]{1,0:T(8,128)(2,1)}, bf16[512,256]{1,0:T(8,128)(2,1)S(1)}, u32[]{:S(2)}) copy-start(bf16[512,256]{1,0:T(8,128)(2,1)S(1)} %get-tuple-element.44.refs_1_.refs_2_) | copy-start | bytes 786436
  28.5 11.3 %collective-permute-start.8 = (bf16[128,1024]{1,0:T(8,128)(2,1)S(1)}, bf16[128,1024]{1,0:T(8,128)(2,1)S(1)}, u32[]{:S(2)}, u32[]{:S(2)}) collective-permute-start(bf16[128,1024]{1,0:T(8,128)(2,1)S(1)} %bitcast.74), channel_id=1, source_target_pairs={{0,2},{1,3},{2,0},{3,1},{4,6},{5,7},{6,4},{7,5},{8,10},{9,11},{10,... | collective-permute-start | bytes 786440 | tf_op jit(solution)/shard_map/ppermute | solution.py:273
  33.8 11.6 %collective-permute-start.10 = (bf16[512,256]{1,0:T(8,128)(2,1)S(1)}, bf16[512,256]{1,0:T(8,128)(2,1)S(1)}, u32[]{:S(2)}, u32[]{:S(2)}) collective-permute-start(bf16[512,256]{1,0:T(8,128)(2,1)S(1)} %get-tuple-element.44.refs_1_.refs_2_), channel_id=1, source_target_pairs={{28,0},{0,4},{4,8},{8,12},{12,16},{16,20},{20,24},{24,28},{29,1},{... | collective-permute-start | bytes 786440 | tf_op jit(solution)/shard_map/ppermute | solution.py:269
  35.4 10.0 %collective-permute-start.5 = (bf16[512,256]{1,0:T(8,128)(2,1)S(1)}, bf16[512,256]{1,0:T(8,128)(2,1)S(1)}, u32[]{:S(2)}, u32[]{:S(2)}) collective-permute-start(bf16[512,256]{1,0:T(8,128)(2,1)S(1)} %get-tuple-element.44.refs_1_.refs_2_), channel_id=1, source_target_pairs={{4,0},{8,4},{12,8},{16,12},{20,16},{24,20},{28,24},{0,28},{5,1},{9... | collective-permute-start | bytes 786440 | tf_op jit(solution)/shard_map/ppermute | solution.py:269
  39.4 9.0 %collective-permute-start.7 = (bf16[128,1024]{1,0:T(8,128)(2,1)S(1)}, bf16[128,1024]{1,0:T(8,128)(2,1)S(1)}, u32[]{:S(2)}, u32[]{:S(2)}) collective-permute-start(bf16[128,1024]{1,0:T(8,128)(2,1)S(1)} %bitcast.75), channel_id=1, source_target_pairs={{0,1},{1,0},{2,3},{3,2},{4,5},{5,4},{6,7},{7,6},{8,9},{9,8},{10,11... | collective-permute-start | bytes 786440 | tf_op jit(solution)/shard_map/ppermute | solution.py:273
  39.8 9.3 %collective-permute-start.9 = (bf16[128,1024]{1,0:T(8,128)(2,1)S(1)}, bf16[128,1024]{1,0:T(8,128)(2,1)S(1)}, u32[]{:S(2)}, u32[]{:S(2)}) collective-permute-start(bf16[128,1024]{1,0:T(8,128)(2,1)S(1)} %collective-permute-done.8.refs_2_), channel_id=1, source_target_pairs={{0,1},{1,0},{2,3},{3,2},{4,5},{5,4},{6,7},{7,6},{8,9},{9,8},{10,11... | collective-permute-start | bytes 786440 | tf_op jit(solution)/shard_map/ppermute | solution.py:273
  39.9 0.7 copy-start.9
  45.4 6.9 %copy-start.5 = (bf16[512,256]{1,0:T(8,128)(2,1)}, bf16[512,256]{1,0:T(8,128)(2,1)S(1)}, u32[]{:S(2)}) copy-start(bf16[512,256]{1,0:T(8,128)(2,1)S(1)} %collective-permute-done.10.refs_3_.refs_1_) | copy-start | bytes 786436
  45.4 9.0 %collective-permute-start.13 = (bf16[512,256]{1,0:T(8,128)(2,1)S(1)}, bf16[512,256]{1,0:T(8,128)(2,1)}, u32[]{:S(2)}, u32[]{:S(2)}) collective-permute-start(bf16[512,256]{1,0:T(8,128)(2,1)S(1)} %collective-permute-done.10.refs_3_.refs_1_), channel_id=1, source_target_pairs={{28,0},{0,4},{4,8},{8,12},{12,16},{16,20},{20,24},{24,28},{29,1},{... | collective-permute-start | bytes 786440 | tf_op jit(solution)/shard_map/ppermute | solution.py:269
  45.4 6.9 %copy-start.7 = (bf16[512,256]{1,0:T(8,128)(2,1)}, bf16[512,256]{1,0:T(8,128)(2,1)S(1)}, u32[]{:S(2)}) copy-start(bf16[512,256]{1,0:T(8,128)(2,1)S(1)} %collective-permute-done.5.refs_2_.refs_0_) | copy-start | bytes 786436
  45.4 9.0 %collective-permute-start.6 = (bf16[512,256]{1,0:T(8,128)(2,1)S(1)}, bf16[512,256]{1,0:T(8,128)(2,1)}, u32[]{:S(2)}, u32[]{:S(2)}) collective-permute-start(bf16[512,256]{1,0:T(8,128)(2,1)S(1)} %collective-permute-done.5.refs_2_.refs_0_), channel_id=1, source_target_pairs={{4,0},{8,4},{12,8},{16,12},{20,16},{24,20},{28,24},{0,28},{5,1},{9... | collective-permute-start | bytes 786440 | tf_op jit(solution)/shard_map/ppermute | solution.py:269
  48.4 0.7 copy-start.11
  49.1 0.7 copy-start.13
  49.8 7.4 %copy-start.16 = (bf16[64,1024]{1,0:T(8,128)(2,1)S(1)}, bf16[64,1024]{1,0:T(8,128)(2,1)}, u32[]{:S(2)}) copy-start(bf16[64,1024]{1,0:T(8,128)(2,1)} %copy-done.15) | copy-start | bytes 393220
  49.8 7.4 %copy-start.18 = (bf16[64,1024]{1,0:T(8,128)(2,1)S(1)}, bf16[64,1024]{1,0:T(8,128)(2,1)}, u32[]{:S(2)}) copy-start(bf16[64,1024]{1,0:T(8,128)(2,1)} %copy-done.17) | copy-start | bytes 393220
  52.3 0.7 copy-start.24
  53.0 0.9 copy-start.26
  54.4 8.2 %collective-permute-start.14 = (bf16[512,256]{1,0:T(8,128)(2,1)}, bf16[512,256]{1,0:T(8,128)(2,1)S(1)}, u32[]{:S(2)}, u32[]{:S(2)}) collective-permute-start(bf16[512,256]{1,0:T(8,128)(2,1)} %collective-permute-done.13.refs_2_.refs_1_), channel_id=1, source_target_pairs={{28,0},{0,4},{4,8},{8,12},{12,16},{16,20},{20,24},{24,28},{29,1},{... | collective-permute-start | bytes 786440 | tf_op jit(solution)/shard_map/ppermute | solution.py:269
  54.4 8.5 %collective-permute-start.11 = (bf16[512,256]{1,0:T(8,128)(2,1)}, bf16[512,256]{1,0:T(8,128)(2,1)S(1)}, u32[]{:S(2)}, u32[]{:S(2)}) collective-permute-start(bf16[512,256]{1,0:T(8,128)(2,1)} %collective-permute-done.6.refs_1_.refs_0_), channel_id=1, source_target_pairs={{4,0},{8,4},{12,8},{16,12},{20,16},{24,20},{28,24},{0,28},{5,1},{9... | collective-permute-start | bytes 786440 | tf_op jit(solution)/shard_map/ppermute | solution.py:269
  57.2 1.0 copy-start.10
  58.2 0.9 copy-start.12
  59.1 0.9 copy-start.14
  60.1 5.6 %copy-start.22 = (s32[4]{0:T(128)S(1)}, s32[4]{0:T(128)}, u32[]{:S(2)}) copy-start(s32[4]{0:T(128)} %constant.73.clone.number_ref) | copy-start | bytes 52
  60.1 5.6 %copy-start.25 = (bf16[512,128]{1,0:T(8,128)(2,1)S(1)}, bf16[512,128]{1,0:T(8,128)(2,1)}, u32[]{:S(2)}) copy-start(bf16[512,128]{1,0:T(8,128)(2,1)} %copy-done.24) | copy-start | bytes 393220
  60.1 5.6 %copy-start.27 = (f32[3,512,128]{2,1,0:T(8,128)S(1)}, f32[3,512,128]{2,1,0:T(8,128)}, u32[]{:S(2)}) copy-start(f32[3,512,128]{2,1,0:T(8,128)} %copy-done.26) | copy-start | bytes 2359300
  62.6 7.0 %collective-permute-start.15 = (bf16[256,256]{1,0:T(8,128)(2,1)S(1)}, bf16[256,256]{1,0:T(8,128)(2,1)S(1)}, u32[]{:S(2)}, u32[]{:S(2)}) collective-permute-start(bf16[256,256]{1,0:T(8,128)(2,1)S(1)} %slice.88), channel_id=1, source_target_pairs={{28,0},{0,4},{4,8},{8,12},{12,16},{16,20},{20,24},{24,28},{29,1},{... | collective-permute-start | bytes 393224 | tf_op jit(solution)/shard_map/ppermute | solution.py:269
  62.9 6.7 %collective-permute-start.12 = (bf16[256,256]{1,0:T(8,128)(2,1)S(1)}, bf16[256,256]{1,0:T(8,128)(2,1)S(1)}, u32[]{:S(2)}, u32[]{:S(2)}) collective-permute-start(bf16[256,256]{1,0:T(8,128)(2,1)S(1)} %slice.87), channel_id=1, source_target_pairs={{4,0},{8,4},{12,8},{16,12},{20,16},{24,20},{28,24},{0,28},{5,1},{9... | collective-permute-start | bytes 393224 | tf_op jit(solution)/shard_map/ppermute | solution.py:269
  70.9 13.2 %collective-permute-start.23 = (bf16[512,128]{1,0:T(8,128)(2,1)S(1)}, bf16[512,128]{1,0:T(8,128)(2,1)S(1)}, u32[]{:S(2)}, u32[]{:S(2)}) collective-permute-start(bf16[512,128]{1,0:T(8,128)(2,1)S(1)} %get-tuple-element.54.a_ref.refs_0_), channel_id=1, source_target_pairs={{0,2},{1,3},{2,0},{3,1},{4,6},{5,7},{6,4},{7,5},{8,10},{9,11},{10,... | collective-permute-start | bytes 393224 | tf_op jit(solution)/shard_map/ppermute | solution.py:273
  71.0 17.6 %collective-permute-start.22 = (bf16[512,128]{1,0:T(8,128)(2,1)S(1)}, bf16[512,128]{1,0:T(8,128)(2,1)S(1)}, u32[]{:S(2)}, u32[]{:S(2)}) collective-permute-start(bf16[512,128]{1,0:T(8,128)(2,1)S(1)} %get-tuple-element.54.a_ref.refs_0_), channel_id=1, source_target_pairs={{0,1},{1,0},{2,3},{3,2},{4,5},{5,4},{6,7},{7,6},{8,9},{9,8},{10,11... | collective-permute-start | bytes 393224 | tf_op jit(solution)/shard_map/ppermute | solution.py:273
  73.6 3.9 %copy-start.21 = (s32[2]{0:T(128)S(1)}, s32[2]{0:T(128)}, u32[]{:S(2)}) copy-start(s32[2]{0:T(128)} %constant.75.clone.number_ref) | copy-start | bytes 28
  74.8 6.4 %collective-permute-start.18 = (bf16[256,256]{1,0:T(8,128)(2,1)S(1)}, bf16[256,256]{1,0:T(8,128)(2,1)S(1)}, u32[]{:S(2)}, u32[]{:S(2)}) collective-permute-start(bf16[256,256]{1,0:T(8,128)(2,1)S(1)} %get-tuple-element.85), channel_id=1, source_target_pairs={{28,0},{0,4},{4,8},{8,12},{12,16},{16,20},{20,24},{24,28},{29,1},{... | collective-permute-start | bytes 393224 | tf_op jit(solution)/shard_map/ppermute | solution.py:269
  74.9 6.3 %collective-permute-start.20 = (bf16[256,256]{1,0:T(8,128)(2,1)S(1)}, bf16[256,256]{1,0:T(8,128)(2,1)S(1)}, u32[]{:S(2)}, u32[]{:S(2)}) collective-permute-start(bf16[256,256]{1,0:T(8,128)(2,1)S(1)} %get-tuple-element.84), channel_id=1, source_target_pairs={{4,0},{8,4},{12,8},{16,12},{20,16},{24,20},{28,24},{0,28},{5,1},{9... | collective-permute-start | bytes 393224 | tf_op jit(solution)/shard_map/ppermute | solution.py:269
  80.2 16.8 %collective-permute-start.16 = (bf16[2,128,1024]{2,1,0:T(8,128)(2,1)S(1)}, bf16[2,128,1024]{2,1,0:T(8,128)(2,1)S(1)}, u32[]{:S(2)}, u32[]{:S(2)}) collective-permute-start(bf16[2,128,1024]{2,1,0:T(8,128)(2,1)S(1)} %get-tuple-element.57), channel_id=1, source_target_pairs={{0,1},{1,0},{2,3},{3,2},{4,5},{5,4},{6,7},{7,6},{8,9},{9,8},{10,11... | collective-permute-start | bytes 1572872 | tf_op jit(solution)/shard_map/ppermute | solution.py:273
  80.9 4.6 %copy-start.20 = (s32[2]{0:T(128)S(1)}, s32[2]{0:T(128)}, u32[]{:S(2)}) copy-start(s32[2]{0:T(128)} %constant.76.clone.number_ref) | copy-start | bytes 28
  81.3 9.2 %collective-permute-start.19 = (bf16[512,256]{1,0:T(8,128)(2,1)S(1)}, bf16[512,256]{1,0:T(8,128)(2,1)S(1)}, u32[]{:S(2)}, u32[]{:S(2)}) collective-permute-start(bf16[512,256]{1,0:T(8,128)(2,1)S(1)} %pad_maximum_fusion.2), channel_id=1, source_target_pairs={{28,0},{0,4},{4,8},{8,12},{12,16},{16,20},{20,24},{24,28},{29,1},{... | collective-permute-start | bytes 786440 | tf_op jit(solution)/shard_map/ppermute | solution.py:269
  82.9 7.6 %collective-permute-start.21 = (bf16[512,256]{1,0:T(8,128)(2,1)S(1)}, bf16[512,256]{1,0:T(8,128)(2,1)S(1)}, u32[]{:S(2)}, u32[]{:S(2)}) collective-permute-start(bf16[512,256]{1,0:T(8,128)(2,1)S(1)} %pad_maximum_fusion.3), channel_id=1, source_target_pairs={{4,0},{8,4},{12,8},{16,12},{20,16},{24,20},{28,24},{0,28},{5,1},{9... | collective-permute-start | bytes 786440 | tf_op jit(solution)/shard_map/ppermute | solution.py:269
  84.1 4.5 %collective-permute-start.24 = (bf16[512,128]{1,0:T(8,128)(2,1)S(1)}, bf16[512,128]{1,0:T(8,128)(2,1)S(1)}, u32[]{:S(2)}, u32[]{:S(2)}) collective-permute-start(bf16[512,128]{1,0:T(8,128)(2,1)S(1)} %collective-permute-done.23.refs_2_), channel_id=1, source_target_pairs={{0,1},{1,0},{2,3},{3,2},{4,5},{5,4},{6,7},{7,6},{8,9},{9,8},{10,11... | collective-permute-start | bytes 393224 | tf_op jit(solution)/shard_map/ppermute | solution.py:273
  90.4 3.0 %copy-start.4 = (bf16[512,256]{1,0:T(8,128)(2,1)S(1)}, bf16[512,256]{1,0:T(8,128)(2,1)}, u32[]{:S(2)}) copy-start(bf16[512,256]{1,0:T(8,128)(2,1)} %copy-done.3) | copy-start | bytes 786436
  90.4 3.0 %copy-start.6 = (bf16[512,256]{1,0:T(8,128)(2,1)S(1)}, bf16[512,256]{1,0:T(8,128)(2,1)}, u32[]{:S(2)}) copy-start(bf16[512,256]{1,0:T(8,128)(2,1)} %copy-done.5) | copy-start | bytes 786436
  90.4 3.0 %copy-start.8 = (bf16[512,256]{1,0:T(8,128)(2,1)S(1)}, bf16[512,256]{1,0:T(8,128)(2,1)}, u32[]{:S(2)}) copy-start(bf16[512,256]{1,0:T(8,128)(2,1)} %copy-done.7) | copy-start | bytes 786436
  90.4 2.9 %copy-start.19 = (s32[3]{0:T(128)S(1)}, s32[3]{0:T(128)}, u32[]{:S(2)}) copy-start(s32[3]{0:T(128)} %constant.77.clone.number_ref) | copy-start | bytes 40
  90.6 8.2 %collective-permute-start.25 = (bf16[512,256]{1,0:T(8,128)(2,1)S(1)}, bf16[512,256]{1,0:T(8,128)(2,1)S(1)}, u32[]{:S(2)}, u32[]{:S(2)}) collective-permute-start(bf16[512,256]{1,0:T(8,128)(2,1)S(1)} %get-tuple-element.79), channel_id=1, source_target_pairs={{28,0},{0,4},{4,8},{8,12},{12,16},{16,20},{20,24},{24,28},{29,1},{... | collective-permute-start | bytes 786440 | tf_op jit(solution)/shard_map/ppermute | solution.py:269
  91.5 7.3 %collective-permute-start.27 = (bf16[512,256]{1,0:T(8,128)(2,1)S(1)}, bf16[512,256]{1,0:T(8,128)(2,1)S(1)}, u32[]{:S(2)}, u32[]{:S(2)}) collective-permute-start(bf16[512,256]{1,0:T(8,128)(2,1)S(1)} %get-tuple-element.78), channel_id=1, source_target_pairs={{4,0},{8,4},{12,8},{16,12},{20,16},{24,20},{28,24},{0,28},{5,1},{9... | collective-permute-start | bytes 786440 | tf_op jit(solution)/shard_map/ppermute | solution.py:269
  97.1 6.5 %collective-permute-start.17 = (bf16[128,1024]{1,0:T(8,128)(2,1)S(1)}, bf16[128,1024]{1,0:T(8,128)(2,1)S(1)}, u32[]{:S(2)}, u32[]{:S(2)}) collective-permute-start(bf16[128,1024]{1,0:T(8,128)(2,1)S(1)} %get-tuple-element.59), channel_id=1, source_target_pairs={{0,2},{1,3},{2,0},{3,1},{4,6},{5,7},{6,4},{7,5},{8,10},{9,11},{10,... | collective-permute-start | bytes 786440 | tf_op jit(solution)/shard_map/ppermute | solution.py:273
  99.0 7.0 %collective-permute-start.26 = (bf16[512,256]{1,0:T(8,128)(2,1)S(1)}, bf16[512,256]{1,0:T(8,128)(2,1)S(1)}, u32[]{:S(2)}, u32[]{:S(2)}) collective-permute-start(bf16[512,256]{1,0:T(8,128)(2,1)S(1)} %get-tuple-element.76), channel_id=1, source_target_pairs={{28,0},{0,4},{4,8},{8,12},{12,16},{16,20},{20,24},{24,28},{29,1},{... | collective-permute-start | bytes 786440 | tf_op jit(solution)/shard_map/ppermute | solution.py:269
  99.1 6.9 %collective-permute-start.28 = (bf16[512,256]{1,0:T(8,128)(2,1)S(1)}, bf16[512,256]{1,0:T(8,128)(2,1)S(1)}, u32[]{:S(2)}, u32[]{:S(2)}) collective-permute-start(bf16[512,256]{1,0:T(8,128)(2,1)S(1)} %get-tuple-element.77), channel_id=1, source_target_pairs={{4,0},{8,4},{12,8},{16,12},{20,16},{24,20},{28,24},{0,28},{5,1},{9... | collective-permute-start | bytes 786440 | tf_op jit(solution)/shard_map/ppermute | solution.py:269
  107.7 15.8 %all-to-all-start.1 = ((bf16[8,128,512]{2,1,0:T(8,128)(2,1)}), bf16[8,128,512]{2,1,0:T(8,128)(2,1)S(1)}, u32[]{:S(2)}, u32[]{:S(2)}) async-start(bf16[8,128,512]{2,1,0:T(8,128)(2,1)} %pad_maximum_fusion), calls=%async_computation.1 | async-start | bytes 2097152 | tf_op jit(solution)/shard_map/all_to_all | solution.py:314
  112.2 4.6 %collective-permute-start.29 = (bf16[2,128,1024]{2,1,0:T(8,128)(2,1)S(1)}, bf16[2,128,1024]{2,1,0:T(8,128)(2,1)S(1)}, u32[]{:S(2)}, u32[]{:S(2)}) collective-permute-start(bf16[2,128,1024]{2,1,0:T(8,128)(2,1)S(1)} %get-tuple-element.71), channel_id=1, source_target_pairs={{0,1},{1,0},{2,3},{3,2},{4,5},{5,4},{6,7},{7,6},{8,9},{9,8},{10,11... | collective-permute-start | bytes 1572872 | tf_op jit(solution)/shard_map/ppermute | solution.py:273
  124.4 13.1 %collective-permute-start.30 = (bf16[128,1024]{1,0:T(8,128)(2,1)S(1)}, bf16[128,1024]{1,0:T(8,128)(2,1)S(1)}, u32[]{:S(2)}, u32[]{:S(2)}) collective-permute-start(bf16[128,1024]{1,0:T(8,128)(2,1)S(1)} %get-tuple-element.74), channel_id=1, source_target_pairs={{0,2},{1,3},{2,0},{3,1},{4,6},{5,7},{6,4},{7,5},{8,10},{9,11},{10,... | collective-permute-start | bytes 786440 | tf_op jit(solution)/shard_map/ppermute | solution.py:273
  125.8 21.0 %all-to-all-start.2 = ((bf16[32,4,512]{2,1,0:T(4,128)(2,1)}), bf16[32,4,512]{2,1,0:T(4,128)(2,1)S(1)}, u32[]{:S(2)}, u32[]{:S(2)}) async-start(bf16[32,4,512]{2,1,0:T(4,128)(2,1)} %clips_sum.1), calls=%async_computation.2 | async-start | bytes 262144 | tf_op jit(solution)/shard_map/all_to_all | solution.py:314
